TPU v7x, 256 devices: a whole 4x4x8 slice. The times are simulated.
256 devices in a mesh: row: 16 (over z, core), col: 16 (over x, y).
Axes of the slice: x: 4, y: 4, z: 8, core: 2. Of those that a mesh axis runs over, the one named last changes fastest.
Arguments:
- wrapped_phase: float32 [32768, 8192], P('row', 'col'), may hold values from -2.85 to 2.85, as said below
Outputs:
- unwrapped: float32 [32768, 8192], P('row', 'col')
Inputs may be any that keep to these rules, and one draw needn't show every extreme that they name: The difference of wrapped_phase between any two adjacent cells of the map lies 0.14 or more away from every odd multiple of pi.
All inputs are finite; a program needn't handle non-finite values.
Results may differ from a plain program's by a relative error of at most 0.0003.
Values sent between devices are 32-bit elements; how exact they have to be, the bound alone decides.
No kernel may reach another device: no remote copies, remote signals or barrier semaphores. Data moves between devices by JAX's collectives and lax.ppermute only.
A program may use at most 128 MiB of HBM per device.

v0:
```python
import math

import jax
import jax.numpy as jnp
import ml_dtypes
import numpy as np
from jax import lax
from jax.experimental import pallas as pl
from jax.experimental.pallas import tpu as pltpu
from jax.sharding import PartitionSpec as P

TILE = 256
TURN = 2.0 * math.pi
PER_TURN = 1.0 / TURN
MAGIC = 1.5 * 2.0**23
ROWS = 8
COLS = 2
WIDTH = COLS * TILE
LANES = 128
PARTS = WIDTH // LANES
LOADS = 8
CHUNK = 16
STEPS = TILE // (2 * CHUNK)
MSG = 48
LOW = 4


def split_terms(table, terms):
    parts, rest = [], np.asarray(table, np.float64)
    for _ in range(terms):
        part = rest.astype(ml_dtypes.bfloat16)
        parts.append(part)
        rest = rest - part.astype(np.float64)
    return parts


def tables():
    q = np.arange(TILE, dtype=np.float64)
    c = np.cos(math.pi * q[:, None] * (2.0 * q[None, :] + 1.0) / (2.0 * TILE))
    c *= math.sqrt(2.0 / TILE)
    c[0] *= math.sqrt(0.5)
    forward = np.concatenate(split_terms(c.T, 3), 0)
    high, low = split_terms(TURN * c, 2)
    backward = np.concatenate([high, high, low], 0)
    mu = 4.0 * np.sin(math.pi * q / (2.0 * TILE)) ** 2
    pivot = [1.0 + mu]
    for _ in range(TILE // 2 - 1):
        pivot.append(2.0 + mu - 1.0 / pivot[-1])
    weights = np.stack([1.0 / d for d in pivot])
    last = pivot[-1]
    even = np.zeros_like(mu)
    even[1:] = 0.5 / (last[1:] - 1.0)
    odd = 0.5 / (last + 1.0)
    middle = np.stack([even, odd])
    freq = np.arange(LOW, dtype=np.float32)
    wave = np.float32(2.0) * np.cos(np.float32(math.pi) * freq / np.float32(TILE))
    held = (wave[:, None] + wave[None, :]).astype(np.float32) - np.float32(4.0)
    exact = mu[:LOW, None] + mu[None, :LOW]
    delta = np.zeros((LOW, LOW))
    known = exact > 0.0
    delta[known] = exact[known] / -held[known].astype(np.float64) - 1.0
    lift = np.zeros((2 * LOW, LANES))
    lift[:LOW, :LOW] = delta
    lift[LOW:, :LOW][known] = delta[known] / exact[known]
    basis = np.zeros((TILE, LANES))
    basis[:, :LOW] = c[:LOW].T
    starts = (delta[0, :LOW] * c[:LOW, 0]) @ c[:LOW]
    ends = (delta[0, :LOW] * c[:LOW, -1]) @ c[:LOW]
    after = lambda g: np.cumsum(g[::-1])[::-1] - g
    edges = np.zeros((8, TILE))
    edges[:4] = np.stack([starts, ends, -TURN * after(starts), -TURN * after(ends)]) / TILE
    low = dict(
        lift=lift.astype(np.float32),
        basis=basis.astype(ml_dtypes.bfloat16),
        waves=c[:LOW, : TILE // 2].astype(np.float32).reshape(-1),
        edges=edges.astype(np.float32),
        steps=edges[:4].astype(np.float32).reshape(-1),
    )
    twice = lambda v: np.concatenate([v, v], 1).astype(np.float32)
    weights = weights.reshape(TILE // 2, 2, LANES).swapaxes(0, 1).astype(np.float32)
    return forward, backward, weights, twice(middle), low


def turns(u):
    return (u + MAGIC) - MAGIC


def lanes(shape):
    return lax.broadcasted_iota(jnp.int32, shape, 1)


def rows_of(shape):
    return lax.broadcasted_iota(jnp.int32, shape, 0)


def fetches(x_ref, xv, sems, spans):
    view = xv.reshape(PARTS, ROWS, TILE, LANES)
    groups = []
    for start, size in spans:
        group = []
        for part in range(PARTS):
            copy = pltpu.make_async_copy(
                x_ref.at[:, pl.ds(start, size), pl.ds(part * LANES, LANES)],
                view.at[part, :, pl.ds(start, size), :],
                sems.at[len(groups) * PARTS + part],
            )
            copy.start()
            group.append(copy)
        groups.append(group)
    return groups


def rows_at(xv, a, parts=PARTS):
    where = pl.ds(a, ROWS, stride=TILE)
    return jnp.concatenate([xv[part, where, :] for part in range(parts)], 1)


def counts_kernel(x_ref, edge_ref, step_ref, msg_ref, loc_ref, xv, sems):
    span = TILE // LOADS
    copies = fetches(x_ref, xv, sems, [(t * span, span) for t in range(LOADS)])
    lane128 = lanes((ROWS, 128))
    zero = jnp.zeros((ROWS, WIDTH), jnp.float32)
    half = jnp.zeros((ROWS, TILE), jnp.float32)
    acc_b, acc_a, acc_aw, acc_z = zero, half, half, zero
    acc_s, acc_e = half, half
    prev = None
    for t in range(LOADS):
        for copy in copies[t]:
            copy.wait()
        if prev is None:
            prev = rows_at(xv, 0, 2) * PER_TURN

        def body(i, carry, t=t):
            acc_b, acc_a, acc_aw, acc_z, acc_s, acc_e, prev, first, last = carry
            a = t * span + i
            z = rows_at(xv, a)
            u = z * PER_TURN
            kb = turns(pltpu.roll(u, WIDTH - 1, axis=1) - u)
            ka = turns(u[:, :TILE] - prev)
            here = lane128 == (a % 128)
            first = jnp.where(here, z[:, 0:1], first)
            last = jnp.where(here, z[:, WIDTH - 1 :], last)
            weight = jnp.asarray(TILE - a, jnp.float32)
            above = jnp.maximum(a - 1, 0)
            left = z[:, :TILE]
            acc_s = acc_s + (step_ref[a] * left + step_ref[2 * TILE + above] * ka)
            acc_e = acc_e + (step_ref[TILE + a] * left + step_ref[3 * TILE + above] * ka)
            return (
                acc_b + kb,
                acc_a + ka,
                acc_aw + weight * ka,
                acc_z + z,
                acc_s,
                acc_e,
                u[:, :TILE],
                first,
                last,
            )

        if t % (LOADS // 2) == 0:
            first = jnp.zeros((ROWS, 128), jnp.float32)
            last = jnp.zeros((ROWS, 128), jnp.float32)
        acc_b, acc_a, acc_aw, acc_z, acc_s, acc_e, prev, first, last = lax.fori_loop(
            0,
            span,
            body,
            (acc_b, acc_a, acc_aw, acc_z, acc_s, acc_e, prev, first, last),
            unroll=8,
        )
        if t % (LOADS // 2) == LOADS // 2 - 1:
            part = t // (LOADS // 2)
            msg_ref[pl.ds(8 * part, 8), :] = first
            msg_ref[pl.ds(16 + 8 * part, 8), :] = last
    z_top = rows_at(xv, 0, 2)
    z_bottom = rows_at(xv, TILE - 1, 2)
    below = pltpu.roll(z_top, ROWS - 1, axis=0)
    seam = turns((below - z_bottom) * PER_TURN)
    seam = jnp.where(rows_of((ROWS, TILE)) == ROWS - 1, 0.0, seam)
    acc_a = acc_a + seam
    lane = lanes((ROWS, WIDTH))
    acc_b = jnp.where(lane == WIDTH - 1, 0.0, acc_b)
    falling = (TILE - 1 - lanes((ROWS, TILE))).astype(jnp.float32) * (1.0 / TILE**2)
    total = lambda v: jnp.sum(v, axis=1, keepdims=True)
    edge = lambda k: edge_ref[k : k + 1, :]
    totals, means = [], []
    for c in range(COLS):
        k, z = (v[:, c * TILE : (c + 1) * TILE] for v in (acc_b, acc_z))
        begin = total(z * edge(0) + k * edge(2))
        end = total(z * edge(1) + k * edge(3))
        totals.append(total(k) * (1.0 / TILE) - (end - begin) * PER_TURN)
        means.append(total(k * falling) + begin * PER_TURN)
    first_total, whole_total = totals[0], totals[0] + totals[1]
    begin, end = total(acc_s), total(acc_e)
    down_total = total(acc_a) * (1.0 / TILE) - (end - begin) * PER_TURN
    down_mean = total(acc_aw) * (1.0 / TILE**2) + begin * PER_TURN
    phase_mean = total(acc_z[:, :TILE]) * (1.0 / TILE**2)
    row = rows_of((ROWS, 128))
    edge = jnp.where(row == 0, z_top[0:1, :128], 0.0)
    edge = jnp.where(row == 1, z_top[0:1, 128:], edge)
    edge = jnp.where(row == 2, z_bottom[ROWS - 1 :, :128], edge)
    edge = jnp.where(row == 3, z_bottom[ROWS - 1 :, 128:], edge)
    msg_ref[pl.ds(32, 8), :] = edge
    values = [whole_total, means[0], down_total, down_mean, phase_mean]
    packed = jnp.zeros((ROWS, 128), jnp.float32)
    for index, value in enumerate(values):
        packed = jnp.where(lane128 == index, value, packed)
    msg_ref[pl.ds(40, 8), :] = packed
    packed = jnp.zeros((ROWS, 128), jnp.float32)
    for index, value in enumerate([first_total, means[0], means[1]]):
        packed = jnp.where(lane128 == index, value, packed)
    loc_ref[...] = packed


def across_kernel(got_ref, loc_ref, down_ref, part_ref):
    me = lax.axis_index("col")
    peers = got_ref.shape[0]
    before = jnp.zeros((ROWS, 1), jnp.float32)
    for peer in range(peers - 1):
        border = jnp.zeros((ROWS, 128), jnp.float32)
        for part in range(2):
            right = got_ref[peer + 1, pl.ds(8 * part, 8), :]
            left = got_ref[peer, pl.ds(16 + 8 * part, 8), :]
            border = border + turns((right - left) * PER_TURN)
        crossed = jnp.sum(border, axis=1, keepdims=True) * (1.0 / TILE)
        both = got_ref[peer, pl.ds(40, 8), 0:1] + crossed
        before = before + jnp.where(peer < me, both, 0.0)
    start = got_ref[0, pl.ds(40, 8), :]
    edge = got_ref[0, pl.ds(32, 8), :]
    loc = loc_ref[...]
    lane = lanes((ROWS, 128))
    row = rows_of((ROWS, 128))
    down = start[:, 2:3]
    down_sum = jnp.sum(down, axis=0, keepdims=True)
    info = jnp.where(lane == 0, down_sum, 0.0)
    info = jnp.where(lane == 1, start[0:1, 3:4], info)
    info = jnp.where(lane == 2, start[0:1, 4:5], info)
    down_ref[...] = jnp.where(row == 4, info, edge)
    here = jnp.zeros((ROWS, 1), jnp.float32)
    for index in range(ROWS - 1):
        here = here + jnp.where(rows_of((ROWS, 1)) > index, down[index : index + 1, :], 0.0)
    shared = before + here - start[:, 1:2] + start[:, 3:4]
    one = shared + loc[:, 1:2]
    two = shared + loc[:, 0:1] + loc[:, 2:3]
    part_ref[...] = jnp.where(lane == 0, one, jnp.where(lane == 1, two, 0.0))


def solve_kernel(
    x_ref, fwd_ref, bwd_ref, w_ref, mid_ref, lift_ref, basis_ref, wave_ref, p_ref, sum_ref, xv, yb, sems
):
    spans = []
    for t in range(STEPS):
        spans += [(CHUNK * t, CHUNK), (TILE - CHUNK * (t + 1), CHUNK)]
    for group in fetches(x_ref, xv, sems, spans):
        for copy in group:
            copy.wait()
    lane = lanes((ROWS, WIDTH))
    closed = (lane == TILE - 1) | (lane == WIDTH - 1)

    def loaded(a):
        return rows_at(xv, a) * PER_TURN

    def sources(start):
        u = loaded(jnp.maximum(start - 1, 0))
        here = loaded(start)
        above = turns(here - u)
        out, own = [], []
        for i in range(CHUNK):
            own.append(here)
            after = loaded(jnp.minimum(start + i + 1, TILE - 1))
            below = turns(after - here)
            kb = jnp.where(closed, 0.0, turns(pltpu.roll(here, WIDTH - 1, axis=1) - here))
            out.append((below - above) + (kb - pltpu.roll(kb, 1, axis=1)))
            here, above = after, below
        return [jnp.concatenate(v, 0).astype(jnp.bfloat16) for v in (out, own)]

    def wave(p, a):
        return wave_ref[p * (TILE // 2) + a]

    def gather_low(low, a, top, bottom):
        even, odd = top + bottom, top - bottom
        return (
            low[0] + even,
            low[1] + wave(1, a) * odd,
            low[2] + wave(2, a) * even,
            low[3] + wave(3, a) * odd,
        )

    def transform(t, low):
        top, own_top = sources(t * CHUNK)
        bottom, own_bottom = sources(TILE - CHUNK * (t + 1))
        stack = lambda u, v: jnp.concatenate([u[:, :TILE], u[:, TILE:], v[:, :TILE], v[:, TILE:]], 0)
        left = stack(own_top, own_bottom)
        own = jnp.dot(left, basis_ref[...], preferred_element_type=jnp.float32)
        piece = lambda k, i: own[(k * CHUNK + i) * ROWS : (k * CHUNK + i + 1) * ROWS]
        for i in range(CHUNK):
            pair = [
                jnp.concatenate([piece(2 * side, j), piece(2 * side + 1, j)], 1)
                for side, j in ((0, i), (1, CHUNK - 1 - i))
            ]
            low = gather_low(low, t * CHUNK + i, *pair)
        left = stack(top, bottom)
        left = jnp.concatenate([left, left, left], 1)
        y = jnp.dot(left, fwd_ref[...], preferred_element_type=jnp.float32)
        size = CHUNK * ROWS
        for side in range(2):
            start = (t * CHUNK if side == 0 else TILE - CHUNK * (t + 1)) * ROWS
            start = pl.multiple_of(start, size)
            for c in range(COLS):
                piece = y[(2 * side + c) * size : (2 * side + c + 1) * size]
                yb[pl.ds(start, size), c * TILE : (c + 1) * TILE] = piece
        return low

    def narrow(v):
        return jnp.concatenate([v[:, c * TILE : c * TILE + LANES] for c in range(COLS)], 1)

    def at(a):
        return pl.ds(pl.multiple_of(a * ROWS, ROWS), ROWS)

    def weight(a):
        pair = [jnp.broadcast_to(w_ref[part, pl.ds(a, 1), :], (ROWS, LANES)) for part in range(2)]
        return jnp.concatenate(pair * COLS, 1)

    def eliminate(t, carry):
        top, bottom, low = carry
        for i in range(CHUNK):
            a = t * CHUNK + i
            scale = weight(jnp.maximum(a - 1, 0))
            own_top, own_bottom = yb[at(a), :], yb[at(TILE - 1 - a), :]
            low = gather_low(low, a, narrow(own_top), narrow(own_bottom))
            top = own_top + scale * top
            bottom = own_bottom + scale * bottom
            yb[at(a), :] = top
            yb[at(TILE - 1 - a), :] = bottom
        return top, bottom, low

    zero = jnp.zeros((ROWS, WIDTH), jnp.float32)
    none = (jnp.zeros((ROWS, COLS * LANES), jnp.float32),) * LOW
    low_z = transform(0, none)

    def forward(t, carry):
        carry, low_z = carry
        carry = eliminate(t - 1, carry)
        return carry, transform(t, low_z)

    carry, low_z = lax.fori_loop(1, STEPS, forward, ((zero, zero, none), low_z))
    top, bottom, low_y = eliminate(STEPS - 1, carry)
    lift = []
    for p in range(LOW):
        rows = [
            jnp.concatenate([lift_ref[k : k + 1, :]] * COLS, 1) for k in (p, LOW + p)
        ]
        lift.append(rows[0] * low_z[p] + rows[1] * low_y[p])
    lift[0] = lift[0] * (1.0 / TILE)
    even = mid_ref[0:1, :] * (top + bottom)
    odd = mid_ref[1:2, :] * (top - bottom)
    mid_top, mid_bottom = even + odd, even - odd

    def substitute(t, carry):
        top, bottom, total = carry
        for i in range(CHUNK):
            a = t * CHUNK + (CHUNK - 1 - i)
            scale = weight(a)
            top = scale * (yb[at(a), :] + top)
            bottom = scale * (yb[at(TILE - 1 - a), :] + bottom)
            even = lift[0] + wave(2, a) * lift[2]
            odd = wave(1, a) * lift[1] + wave(3, a) * lift[3]
            for low, value, row in ((even + odd, top, a), (even - odd, bottom, TILE - 1 - a)):
                for part in range(PARTS):
                    piece = value[:, part * LANES : (part + 1) * LANES]
                    if part % 2 == 0:
                        piece = piece + low[:, part // 2 * LANES : (part // 2 + 1) * LANES]
                    yb[at(row), part * LANES : (part + 1) * LANES] = piece
            total = total + narrow(top + bottom)
        return top, bottom, total

    def restore(t):
        size = CHUNK * ROWS
        pieces, starts = [], []
        for side in range(2):
            first = t * CHUNK if side == 0 else TILE - CHUNK * (t + 1)
            starts.append(first)
            block = yb[pl.ds(pl.multiple_of(first * ROWS, size), size), :]
            for c in range(COLS):
                pieces.append(block[:, c * TILE : (c + 1) * TILE])
        value = jnp.concatenate(pieces, 0)
        high = value.astype(jnp.bfloat16)
        low = (value - high.astype(jnp.float32)).astype(jnp.bfloat16)
        left = jnp.concatenate([high, low, high], 1)
        y = jnp.dot(left, bwd_ref[...], preferred_element_type=jnp.float32)
        for side in range(2):
            for i in range(CHUNK):
                where = pl.ds(starts[side] + i, ROWS, stride=TILE)
                for part in range(PARTS):
                    from_row = (2 * side + part // 2) * size + i * ROWS
                    from_lane = (part % 2) * LANES
                    piece = y[from_row : from_row + ROWS, from_lane : from_lane + LANES]
                    p_ref[part, where, :] = xv[part, where, :] + piece

    carry = substitute(STEPS - 1, (mid_bottom, mid_top, none[0]))

    def backward(i, carry):
        t = STEPS - 2 - i
        carry = substitute(t, carry)
        restore(t + 1)
        return carry

    _, _, total = lax.fori_loop(0, STEPS - 1, backward, carry)
    restore(0)
    sum_ref[...] = total


def finish_kernel(p_ref, sum_ref, part_ref, down_ref, out_ref, stage, sems):
    me = lax.axis_index("row")
    peers = down_ref.shape[0]
    before = jnp.zeros((1, 1), jnp.float32)
    for peer in range(peers - 1):
        border = turns((down_ref[peer + 1, 0:2, :] - down_ref[peer, 2:4, :]) * PER_TURN)
        border = jnp.sum(jnp.sum(border, axis=1, keepdims=True), axis=0, keepdims=True)
        both = border * (1.0 / TILE) + down_ref[peer, 4:5, 0:1]
        before = before + jnp.where(peer < me, both, 0.0)
    shared = before - down_ref[0, 4:5, 1:2]
    mean = down_ref[0, 4:5, 2:3]
    shift = []
    for c in range(COLS):
        level = sum_ref[:, c * LANES : c * LANES + 1] * (1.0 / (16.0 * TILE))
        value = -mean - TURN * (part_ref[:, c : c + 1] + shared + level)
        shift.append(jnp.broadcast_to(value, (ROWS, LANES)))
    copies = []
    for row in range(ROWS):
        rows = pl.ds(row * TILE, TILE)
        for part in range(PARTS):
            cols = slice(part * LANES, (part + 1) * LANES)
            stage[rows, cols] = p_ref[part, rows, :] + shift[part // 2][row : row + 1, :]
        copy = pltpu.make_async_copy(stage.at[rows, :], out_ref.at[rows, :], sems.at[row])
        copy.start()
        copies.append(copy)
    for copy in copies:
        copy.wait()


VMEM = pl.BlockSpec(memory_space=pltpu.VMEM)
HBM = pl.BlockSpec(memory_space=pltpu.HBM)
SMEM = pl.BlockSpec(memory_space=pltpu.SMEM)


def f32(*shape):
    return jax.ShapeDtypeStruct(shape, jnp.float32)


def to_all(x, axis):
    peers = lax.axis_size(axis)
    return lax.all_to_all(jnp.broadcast_to(x[None], (peers, *x.shape)), axis, 0, 0, tiled=True)


def per_device(phase):
    *big, low = tables()
    forward, backward, weights, middle = (jnp.asarray(t) for t in big)
    low = {k: jnp.asarray(v) for k, v in low.items()}
    grid = pltpu.with_memory_space_constraint(phase.reshape(ROWS, TILE, WIDTH), pltpu.HBM)
    msg, loc = pl.pallas_call(
        counts_kernel,
        out_shape=(f32(MSG, 128), f32(ROWS, 128)),
        in_specs=[HBM, VMEM, SMEM],
        out_specs=(VMEM, VMEM),
        scratch_shapes=[
            pltpu.VMEM((PARTS, ROWS * TILE, LANES), jnp.float32),
            pltpu.SemaphoreType.DMA((LOADS * PARTS,)),
        ],
        compiler_params=pltpu.CompilerParams(vmem_limit_bytes=8 << 20),
        cost_estimate=pl.CostEstimate(flops=1 << 24, bytes_accessed=4 << 20, transcendentals=0),
        name="counts",
    )(grid, low["edges"], low["steps"])
    got = to_all(msg, "col")
    down, part = pl.pallas_call(
        across_kernel,
        out_shape=(f32(ROWS, 128), f32(ROWS, 128)),
        in_specs=[VMEM, VMEM],
        out_specs=(VMEM, VMEM),
        name="across",
    )(got, loc)
    downs = to_all(down, "row")
    p, total = pl.pallas_call(
        solve_kernel,
        out_shape=(f32(PARTS, ROWS * TILE, LANES), f32(ROWS, COLS * LANES)),
        in_specs=[HBM, VMEM, VMEM, VMEM, VMEM, VMEM, VMEM, SMEM],
        out_specs=(VMEM, VMEM),
        scratch_shapes=[
            pltpu.VMEM((PARTS, ROWS * TILE, LANES), jnp.float32),
            pltpu.VMEM((ROWS * TILE, WIDTH), jnp.float32),
            pltpu.SemaphoreType.DMA((2 * STEPS * PARTS,)),
        ],
        compiler_params=pltpu.CompilerParams(vmem_limit_bytes=14 << 20),
        cost_estimate=pl.CostEstimate(flops=4 << 30, bytes_accessed=8 << 20, transcendentals=0),
        name="solve",
    )(grid, forward, backward, weights, middle, low["lift"], low["basis"], low["waves"])
    return pl.pallas_call(
        finish_kernel,
        out_shape=f32(ROWS * TILE, WIDTH),
        in_specs=[VMEM, VMEM, VMEM, VMEM],
        out_specs=HBM,
        scratch_shapes=[
            pltpu.VMEM((ROWS * TILE, WIDTH), jnp.float32),
            pltpu.SemaphoreType.DMA((ROWS,)),
        ],
        compiler_params=pltpu.CompilerParams(vmem_limit_bytes=8 << 20),
        name="finish",
    )(pltpu.with_memory_space_constraint(p, pltpu.VMEM), total, part, downs)


def solution(mesh):
    return jax.shard_map(
        per_device, mesh=mesh, in_specs=(P("row", "col"),), out_specs=P("row", "col"), check_vma=False
    )
```

profile of v0, /device:TPU:1, one launch (start us, length us, event | category | flops | bytes accessed | tf_op | source)
XLA Modules:
  0.0 68.1 jit_solution(4554085053609417208)
XLA Ops:
  0.0 0.0 copy-start.12
  0.0 0.0 copy-start.10
  0.0 0.0 copy-start.11
  0.0 0.0 copy-start.2
  0.0 0.7 %copy-done.2 = f32[8,256]{1,0:T(8,128)S(1)} copy-done((f32[8,256]{1,0:T(8,128)S(1)}, f32[8,256]{1,0:T(8,128)}, u32[]{:S(2)}) %copy-start.2) | copy-done | bytes 8216
  0.7 0.0 copy-start.4
  0.7 0.7 %copy-done.4 = f32[1024]{0:T(1024)S(1)} copy-done((f32[1024]{0:T(1024)S(1)}, f32[1024]{0:T(1024)}, u32[]{:S(2)}) %copy-start.4) | copy-done | bytes 4120
  1.4 0.0 copy-start.6
  1.4 0.0 copy-start.7
  1.4 0.0 copy-start.8
  1.4 0.0 copy-start.9
  1.4 8.0 %counts.1 = (f32[48,128]{1,0:T(8,128)S(1)}, f32[8,128]{1,0:T(8,128)S(1)}) custom-call(f32[8,256,512]{2,1,0:T(8,128)} %bitcast.1, f32[8,256]{1,0:T(8,128)S(1)} %copy-done.2, f32[1024]{0:T(1024)S(1)} %copy-done.4), custom_call_target="tpu_custom_call" | custom-call | flops 16777216 | bytes 4194304 | tf_op jit(solution)/shard_map/counts/pallas_call | solution.py:460
  9.5 0.0 copy-start.5
  9.5 0.6 copy-done.5
  10.1 15.8 %all_to_all.10.got_ref = f32[16,48,128]{2,1,0:T(8,128)} all-to-all(f32[16,48,128]{2,1,0:T(8,128)S(1)} %broadcast_in_dim.4), channel_id=1, replica_groups=mesh['row'=16,'col'=16] {'col'}, dimensions={0} | all-to-all | bytes 786432 | tf_op jit(solution)/shard_map/all_to_all | solution.py:452
  25.8 1.8 %across.1 = (f32[8,128]{1,0:T(8,128)}, f32[8,128]{1,0:T(8,128)}) custom-call(f32[16,48,128]{2,1,0:T(8,128)} %all_to_all.10.got_ref, f32[8,128]{1,0:T(8,128)} %copy-done.5), custom_call_target="tpu_custom_call" | custom-call | tf_op jit(solution)/shard_map/across/pallas_call | solution.py:474
  27.6 1.3 %broadcast_in_dim.5 = f32[16,8,128]{2,1,0:T(8,128)} broadcast(f32[8,128]{1,0:T(8,128)} %get-tuple-element.16), dimensions={1,2} | broadcast | bytes 69632 | tf_op jit(solution)/shard_map/broadcast_in_dim | solution.py:452
  28.9 11.0 %all-to-all-start.1 = ((f32[16,8,128]{2,1,0:T(8,128)}), f32[16,8,128]{2,1,0:T(8,128)S(1)}, u32[]{:S(2)}, u32[]{:S(2)}) async-start(f32[16,8,128]{2,1,0:T(8,128)} %broadcast_in_dim.5), calls=%async_computation.1 | async-start | bytes 131072 | tf_op jit(solution)/shard_map/all_to_all | solution.py:452
  39.9 0.0 copy-done.12
  39.9 0.0 copy-done.10
  40.0 0.0 copy-done.11
  40.0 0.0 copy-done.6
  40.0 0.0 copy-done.7
  40.0 0.0 copy-done.8
  40.0 0.0 copy-done.9
  40.0 0.0 copy-start.3
  40.0 21.5 %solve.1 = (f32[4,2048,128]{2,1,0:T(8,128)S(1)}, f32[8,256]{1,0:T(8,128)S(1)}) custom-call(f32[8,256,512]{2,1,0:T(8,128)} %bitcast.2, bf16[768,256]{1,0:T(8,128)(2,1)S(1)} %copy-done.7, bf16[768,256]{1,0:T(8,128)(2,1)S(1)} %copy-done.6, f32[2,128,128]{2,1,0:T(8,128)S(1)} %copy-done.8, f32[2,512]{1,0:T(2,128)S(1)} %copy-done.11, f32[8,128]{1,0:T(8,128)S(1)} %copy-done.10, ...), custom_call_target="tpu_custom_call" | custom-call | flops 4294967296 | bytes 8388608 | tf_op jit(solution)/shard_map/solve/pallas_call | solution.py:482
  61.5 0.0 copy-start
  61.5 2.0 %copy-done = f32[4,2048,128]{2,1,0:T(8,128)} copy-done((f32[4,2048,128]{2,1,0:T(8,128)}, f32[4,2048,128]{2,1,0:T(8,128)S(1)}, u32[]{:S(2)}) %copy-start) | copy-done | bytes 4194328
  63.5 0.0 all-to-all-done.1.down_ref
  63.5 0.0 copy-done.3
  63.5 0.0 copy-start.1
  63.5 2.2 %copy-done.1 = f32[4,2048,128]{2,1,0:T(8,128)S(1)} copy-done((f32[4,2048,128]{2,1,0:T(8,128)S(1)}, f32[4,2048,128]{2,1,0:T(8,128)}, u32[]{:S(2)}) %copy-start.1) | copy-done | bytes 4194328
  65.7 2.5 %finish.1 = f32[2048,512]{1,0:T(8,128)} custom-call(f32[4,2048,128]{2,1,0:T(8,128)S(1)} %copy-done.1, f32[8,256]{1,0:T(8,128)S(1)} %get-tuple-element.12.sum_ref, f32[8,128]{1,0:T(8,128)S(1)} %copy-done.3, f32[16,8,128]{2,1,0:T(8,128)S(1)} %all-to-all-done.1.down_ref), custom_call_target="tpu_custom_call" | custom-call | tf_op jit(solution)/shard_map/finish/pallas_call | solution.py:496
  (1 shorter events, 0.0 us)
Async XLA Ops:
  0.0 39.9 %copy-start.12 = (f32[512]{0:T(512)S(1)}, f32[512]{0:T(512)}, u32[]{:S(2)}) copy-start(f32[512]{0:T(512)} %constant.24.clone.wave_ref) | copy-start | bytes 6148
  0.0 39.9 %copy-start.10 = (f32[8,128]{1,0:T(8,128)S(1)}, f32[8,128]{1,0:T(8,128)}, u32[]{:S(2)}) copy-start(f32[8,128]{1,0:T(8,128)} %constant.22.clone.lift_ref) | copy-start | bytes 12292
  0.0 39.9 %copy-start.11 = (f32[2,512]{1,0:T(2,128)S(1)}, f32[2,512]{1,0:T(2,128)}, u32[]{:S(2)}) copy-start(f32[2,512]{1,0:T(2,128)} %constant.21.clone.mid_ref) | copy-start | bytes 12292
  0.0 0.7 %copy-start.2 = (f32[8,256]{1,0:T(8,128)S(1)}, f32[8,256]{1,0:T(8,128)}, u32[]{:S(2)}) copy-start(f32[8,256]{1,0:T(8,128)} %constant.25.clone.edge_ref) | copy-start | bytes 24580
  0.7 0.7 %copy-start.4 = (f32[1024]{0:T(1024)S(1)}, f32[1024]{0:T(1024)}, u32[]{:S(2)}) copy-start(f32[1024]{0:T(1024)} %constant.26.clone.step_ref) | copy-start | bytes 12292
  1.4 38.5 %copy-start.6 = (bf16[768,256]{1,0:T(8,128)(2,1)S(1)}, bf16[768,256]{1,0:T(8,128)(2,1)}, u32[]{:S(2)}) copy-start(bf16[768,256]{1,0:T(8,128)(2,1)} %constant.19.clone.bwd_ref) | copy-start | bytes 1179652
  1.4 38.5 %copy-start.7 = (bf16[768,256]{1,0:T(8,128)(2,1)S(1)}, bf16[768,256]{1,0:T(8,128)(2,1)}, u32[]{:S(2)}) copy-start(bf16[768,256]{1,0:T(8,128)(2,1)} %constant.18.clone.fwd_ref) | copy-start | bytes 1179652
  1.4 38.5 %copy-start.8 = (f32[2,128,128]{2,1,0:T(8,128)S(1)}, f32[2,128,128]{2,1,0:T(8,128)}, u32[]{:S(2)}) copy-start(f32[2,128,128]{2,1,0:T(8,128)} %constant.20.clone.w_ref) | copy-start | bytes 393220
  1.4 38.6 %copy-start.9 = (bf16[256,128]{1,0:T(8,128)(2,1)S(1)}, bf16[256,128]{1,0:T(8,128)(2,1)}, u32[]{:S(2)}) copy-start(bf16[256,128]{1,0:T(8,128)(2,1)} %constant.23.clone.basis_ref) | copy-start | bytes 196612
  9.5 0.6 copy-start.5
  28.9 34.5 %all-to-all-start.1 = ((f32[16,8,128]{2,1,0:T(8,128)}), f32[16,8,128]{2,1,0:T(8,128)S(1)}, u32[]{:S(2)}, u32[]{:S(2)}) async-start(f32[16,8,128]{2,1,0:T(8,128)} %broadcast_in_dim.5), calls=%async_computation.1 | async-start | bytes 131072 | tf_op jit(solution)/shard_map/all_to_all | solution.py:452
  40.0 23.5 %copy-start.3 = (f32[8,128]{1,0:T(8,128)S(1)}, f32[8,128]{1,0:T(8,128)}, u32[]{:S(2)}) copy-start(f32[8,128]{1,0:T(8,128)} %get-tuple-element.15.part_ref) | copy-start | bytes 12292
  61.5 2.0 %copy-start = (f32[4,2048,128]{2,1,0:T(8,128)}, f32[4,2048,128]{2,1,0:T(8,128)S(1)}, u32[]{:S(2)}) copy-start(f32[4,2048,128]{2,1,0:T(8,128)S(1)} %get-tuple-element.11.p_ref) | copy-start | bytes 12582916
  63.5 2.2 %copy-start.1 = (f32[4,2048,128]{2,1,0:T(8,128)S(1)}, f32[4,2048,128]{2,1,0:T(8,128)}, u32[]{:S(2)}) copy-start(f32[4,2048,128]{2,1,0:T(8,128)} %copy-done) | copy-start | bytes 12582916
where the time goes:
time: 68.5 us; the launch traced here: 68.1 us
  Pallas kernels  33.7 us (49%)
  blocking collectives  15.8 us (23%)
  starting transfers between devices  11 us (16%)
  local copies, waits for them, and re-layouts  7.57 us (11%)
    pallas_call x1, Pallas kernels, per_device(): pl.pallas_call(solve_kernel, out_shape=(f32(PARTS, ROWS * TILE, LANES), f...  21.5 us
    all_to_all x1, blocking collectives, to_all(): lax.all_to_all(jnp.broadcast_to(x[None], (peers, *x.shape)), axis, 0, 0,...  15.8 us
    all_to_all x1, starting transfers between devices, to_all(): lax.all_to_all(jnp.broadcast_to(x[None], (peers, *x.shape)), axis, 0, 0,...  11 us
    pallas_call x1, Pallas kernels, per_device(): pl.pallas_call(counts_kernel, out_shape=(f32(MSG, 128), f32(ROWS, 128)),...  8 us
    unnamed x26, local copies, waits for them, and re-layouts  6.23 us
    pallas_call x1, Pallas kernels, per_device(): pl.pallas_call(finish_kernel, out_shape=f32(ROWS * TILE, WIDTH), in_specs...  2.45 us
    pallas_call x1, Pallas kernels, per_device(): pl.pallas_call(across_kernel, out_shape=(f32(ROWS, 128), f32(ROWS, 128)),...  1.79 us
  transfers between devices with their start and end apart: 1, of which 0 were waited for; matrix products, arithmetic and copies ran while one was open for 0% of the time, Pallas kernels for 32%

commit v1 on v0

v1 whole, which is shorter than its diff:
```python
import math

import jax
import jax.numpy as jnp
import ml_dtypes
import numpy as np
from jax import lax
from jax.experimental import pallas as pl
from jax.experimental.pallas import tpu as pltpu
from jax.sharding import PartitionSpec as P

TILE = 256
TURN = 2.0 * math.pi
PER_TURN = 1.0 / TURN
MAGIC = 1.5 * 2.0**23
ROWS = 8
COLS = 2
WIDTH = COLS * TILE
LANES = 128
PARTS = WIDTH // LANES
PITCH = TILE + 8
LOADS = 8
CHUNK = 16
STEPS = TILE // (2 * CHUNK)
MSG = 48
LOW = 4


def split_terms(table, terms):
    parts, rest = [], np.asarray(table, np.float64)
    for _ in range(terms):
        part = rest.astype(ml_dtypes.bfloat16)
        parts.append(part)
        rest = rest - part.astype(np.float64)
    return parts


def tables():
    q = np.arange(TILE, dtype=np.float64)
    c = np.cos(math.pi * q[:, None] * (2.0 * q[None, :] + 1.0) / (2.0 * TILE))
    c *= math.sqrt(2.0 / TILE)
    c[0] *= math.sqrt(0.5)
    step = np.zeros_like(c.T)
    step[:-1] = c.T[:-1] - c.T[1:]
    forward = np.concatenate(split_terms(c.T, 2) + split_terms(step, 2), 0)
    across = np.zeros((TILE, TILE))
    index = np.arange(TILE - 1)
    across[index + 1, index], across[index, index] = 1.0, -1.0
    high, low = split_terms(TURN * c, 2)
    backward = np.concatenate([high, high, low], 0)
    mu = 4.0 * np.sin(math.pi * q / (2.0 * TILE)) ** 2
    pivot = [1.0 + mu]
    for _ in range(TILE // 2 - 1):
        pivot.append(2.0 + mu - 1.0 / pivot[-1])
    weights = np.stack([1.0 / d for d in pivot])
    last = pivot[-1]
    even = np.zeros_like(mu)
    even[1:] = 0.5 / (last[1:] - 1.0)
    odd = 0.5 / (last + 1.0)
    middle = np.stack([even, odd])
    freq = np.arange(LOW, dtype=np.float32)
    wave = np.float32(2.0) * np.cos(np.float32(math.pi) * freq / np.float32(TILE))
    held = (wave[:, None] + wave[None, :]).astype(np.float32) - np.float32(4.0)
    exact = mu[:LOW, None] + mu[None, :LOW]
    delta = np.zeros((LOW, LOW))
    known = exact > 0.0
    delta[known] = exact[known] / -held[known].astype(np.float64) - 1.0
    lift = np.zeros((2 * LOW, LANES))
    lift[:LOW, :LOW] = delta
    lift[LOW:, :LOW][known] = delta[known] / exact[known]
    basis = np.zeros((TILE, LANES))
    basis[:, :LOW] = c[:LOW].T
    starts = (delta[0, :LOW] * c[:LOW, 0]) @ c[:LOW]
    ends = (delta[0, :LOW] * c[:LOW, -1]) @ c[:LOW]
    after = lambda g: np.cumsum(g[::-1])[::-1] - g
    edges = np.zeros((8, TILE))
    edges[:4] = np.stack([starts, ends, -TURN * after(starts), -TURN * after(ends)]) / TILE
    low = dict(
        lift=lift.astype(np.float32),
        basis=np.concatenate([across, basis], 1).astype(ml_dtypes.bfloat16),
        across=across.astype(ml_dtypes.bfloat16),
        waves=c[:LOW, : TILE // 2].astype(np.float32).reshape(-1),
        edges=edges.astype(np.float32),
        steps=edges[:4].astype(np.float32).reshape(-1),
    )
    twice = lambda v: np.concatenate([v, v], 1).astype(np.float32)
    weights = weights.reshape(TILE // 2, 2, LANES).swapaxes(0, 1).astype(np.float32)
    return forward, backward, weights, twice(middle), low


def turns(u):
    return (u + MAGIC) - MAGIC


def lanes(shape):
    return lax.broadcasted_iota(jnp.int32, shape, 1)


def rows_of(shape):
    return lax.broadcasted_iota(jnp.int32, shape, 0)


def span_copies(x_ref, xv, sems, start, size, t):
    view = xv.reshape(PARTS, ROWS, PITCH, LANES)
    copies = []
    for part in range(PARTS):
        ends = (
            x_ref.at[:, pl.ds(start, size), pl.ds(part * LANES, LANES)],
            view.at[part, :, pl.ds(start, size), :],
        )
        copies.append(pltpu.make_async_copy(*ends, sems.at[t * PARTS + part]))
    return copies


def side_start(t, side):
    start = CHUNK * t if side == 0 else TILE - CHUNK * (t + 1)
    return start if isinstance(start, int) else pl.multiple_of(start, CHUNK)


def field_copies(x_ref, xv, sems, t, out=False):
    view = xv.reshape(PARTS, ROWS, PITCH, LANES)
    copies = []
    for side in range(2):
        for part in range(PARTS):
            span = pl.ds(side_start(t, side), CHUNK)
            ends = (x_ref.at[:, span, pl.ds(part * LANES, LANES)], view.at[part, :, span, :])
            sem = sems.at[(2 * t + side) * PARTS + part]
            copies.append(pltpu.make_async_copy(*(ends[::-1] if out else ends), sem))
    return copies


def row_copies(y_ref, yb, sems, t, out=False):
    copies = []
    for side in range(2):
        span = pl.ds(side_start(t, side) * ROWS, CHUNK * ROWS)
        ends = (y_ref.at[span, :], yb.at[span, :])
        copies.append(pltpu.make_async_copy(*(ends[::-1] if out else ends), sems.at[2 * t + side]))
    return copies


def start_all(copies):
    for copy in copies:
        copy.start()


def wait_all(copies):
    for copy in copies:
        copy.wait()


def rows_at(xv, a, parts=PARTS):
    where = pl.ds(a, ROWS, stride=PITCH)
    return jnp.concatenate([xv[part, where, :] for part in range(parts)], 1)


def counts_kernel(
    x_ref, edge_hbm, step_hbm, across_hbm, all_ref, loc_ref,
    msg_ref, xv, edge_ref, step_ref, across_ref, sems, table_sems
):
    tables_in = [
        pltpu.make_async_copy(step_hbm, step_ref, table_sems.at[0]),
        pltpu.make_async_copy(edge_hbm, edge_ref, table_sems.at[1]),
        pltpu.make_async_copy(across_hbm, across_ref, table_sems.at[2]),
    ]
    for copy in tables_in:
        copy.start()
    span = TILE // LOADS
    for t in range(LOADS):
        start_all(span_copies(x_ref, xv, sems, t * span, span, t))
    for copy in tables_in:
        copy.wait()
    lane128 = lanes((ROWS, 128))
    zero = jnp.zeros((ROWS, WIDTH), jnp.float32)
    half = jnp.zeros((ROWS, TILE), jnp.float32)
    acc_b, acc_a, acc_aw, acc_z = zero, half, half, zero
    acc_s, acc_e = half, half
    msg_ref[...] = jnp.zeros((MSG, LANES), jnp.float32)

    def chunk(t, carry):
        acc_b, acc_m, acc_a, acc_aw, acc_z, acc_s, acc_e, prev = carry

        wait_all(span_copies(x_ref, xv, sems, pl.multiple_of(t * span, span), span, t))
        half = t // (LOADS // 2)
        near = pl.ds(pl.multiple_of(8 * half, 8), 8)
        far = pl.ds(pl.multiple_of(16 + 8 * half, 8), 8)
        first, last = msg_ref[near, :], msg_ref[far, :]
        own = []
        for i in range(span):
            a = t * span + i
            z = rows_at(xv, a)
            u = z * PER_TURN
            own.append(u)
            if i == 0:
                prev = jnp.where(t == 0, u[:, :TILE], prev)
            ka = turns(u[:, :TILE] - prev)
            edge = pltpu.roll(u[:, TILE - LANES : TILE], 1, axis=1)
            acc_m = acc_m + turns(u[:, TILE : TILE + LANES] - edge)
            here = lane128 == (a % LANES)
            first = jnp.where(here, z[:, 0:1], first)
            last = jnp.where(here, z[:, WIDTH - 1 :], last)
            weight = (TILE - a).astype(jnp.float32)
            above = jnp.maximum(a - 1, 0)
            left = z[:, :TILE]
            acc_s = acc_s + (step_ref[a] * left + step_ref[2 * TILE + above] * ka)
            acc_e = acc_e + (step_ref[TILE + a] * left + step_ref[3 * TILE + above] * ka)
            acc_a = acc_a + ka
            acc_aw = acc_aw + weight * ka
            acc_z = acc_z + z
            prev = u[:, :TILE]
        msg_ref[near, :] = first
        msg_ref[far, :] = last
        own = jnp.concatenate(own, 0).astype(jnp.bfloat16)
        own = jnp.concatenate([own[:, :TILE], own[:, TILE:]], 0)
        kb = turns(jnp.dot(own, across_ref[...], preferred_element_type=jnp.float32))
        for i in range(span):
            pair = [kb[(c * span + i) * ROWS : (c * span + i + 1) * ROWS] for c in range(COLS)]
            acc_b = acc_b + jnp.concatenate(pair, 1)
        return acc_b, acc_m, acc_a, acc_aw, acc_z, acc_s, acc_e, prev

    start = (acc_b, jnp.zeros((ROWS, LANES), jnp.float32), acc_a, acc_aw, acc_z, acc_s, acc_e, half)
    acc_b, acc_m, acc_a, acc_aw, acc_z, acc_s, acc_e, _ = lax.fori_loop(0, LOADS, chunk, start
    )
    z_top = rows_at(xv, 0, 2)
    z_bottom = rows_at(xv, TILE - 1, 2)
    below = pltpu.roll(z_top, ROWS - 1, axis=0)
    seam = turns((below - z_bottom) * PER_TURN)
    seam = jnp.where(rows_of((ROWS, TILE)) == ROWS - 1, 0.0, seam)
    acc_a = acc_a + seam
    falling = (TILE - 1 - lanes((ROWS, TILE))).astype(jnp.float32) * (1.0 / TILE**2)
    total = lambda v: jnp.sum(v, axis=1, keepdims=True)
    edge = lambda k: edge_ref[k : k + 1, :]
    totals, means = [], []
    for c in range(COLS):
        k, z = (v[:, c * TILE : (c + 1) * TILE] for v in (acc_b, acc_z))
        begin = total(z * edge(0) + k * edge(2))
        end = total(z * edge(1) + k * edge(3))
        totals.append(total(k) * (1.0 / TILE) - (end - begin) * PER_TURN)
        means.append(total(k * falling) + begin * PER_TURN)
    totals[0] = totals[0] + acc_m[:, 0:1] * (1.0 / TILE)
    first_total, whole_total = totals[0], totals[0] + totals[1]
    begin, end = total(acc_s), total(acc_e)
    down_total = total(acc_a) * (1.0 / TILE) - (end - begin) * PER_TURN
    down_mean = total(acc_aw) * (1.0 / TILE**2) + begin * PER_TURN
    phase_mean = total(acc_z[:, :TILE]) * (1.0 / TILE**2)
    row = rows_of((ROWS, 128))
    edge = jnp.where(row == 0, z_top[0:1, :128], 0.0)
    edge = jnp.where(row == 1, z_top[0:1, 128:], edge)
    edge = jnp.where(row == 2, z_bottom[ROWS - 1 :, :128], edge)
    edge = jnp.where(row == 3, z_bottom[ROWS - 1 :, 128:], edge)
    msg_ref[pl.ds(32, 8), :] = edge
    values = [whole_total, means[0], down_total, down_mean, phase_mean]
    packed = jnp.zeros((ROWS, 128), jnp.float32)
    for index, value in enumerate(values):
        packed = jnp.where(lane128 == index, value, packed)
    msg_ref[pl.ds(40, 8), :] = packed
    packed = jnp.zeros((ROWS, 128), jnp.float32)
    for index, value in enumerate([first_total, means[0], means[1]]):
        packed = jnp.where(lane128 == index, value, packed)
    loc_ref[...] = packed
    for peer in range(all_ref.shape[0]):
        all_ref[peer] = msg_ref[...]


def across_kernel(got_ref, loc_ref, down_ref, part_ref):
    me = lax.axis_index("col")
    peers = got_ref.shape[0]
    before = jnp.zeros((ROWS, 1), jnp.float32)
    for peer in range(peers - 1):
        border = jnp.zeros((ROWS, 128), jnp.float32)
        for part in range(2):
            right = got_ref[peer + 1, pl.ds(8 * part, 8), :]
            left = got_ref[peer, pl.ds(16 + 8 * part, 8), :]
            border = border + turns((right - left) * PER_TURN)
        crossed = jnp.sum(border, axis=1, keepdims=True) * (1.0 / TILE)
        both = got_ref[peer, pl.ds(40, 8), 0:1] + crossed
        before = before + jnp.where(peer < me, both, 0.0)
    start = got_ref[0, pl.ds(40, 8), :]
    edge = got_ref[0, pl.ds(32, 8), :]
    loc = loc_ref[...]
    lane = lanes((ROWS, 128))
    row = rows_of((ROWS, 128))
    down = start[:, 2:3]
    down_sum = jnp.sum(down, axis=0, keepdims=True)
    info = jnp.where(lane == 0, down_sum, 0.0)
    info = jnp.where(lane == 1, start[0:1, 3:4], info)
    info = jnp.where(lane == 2, start[0:1, 4:5], info)
    info = jnp.where(row == 4, info, edge)
    for peer in range(down_ref.shape[0]):
        down_ref[peer] = info
    here = jnp.zeros((ROWS, 1), jnp.float32)
    for index in range(ROWS - 1):
        here = here + jnp.where(rows_of((ROWS, 1)) > index, down[index : index + 1, :], 0.0)
    shared = before + here - start[:, 1:2] + start[:, 3:4]
    one = shared + loc[:, 1:2]
    two = shared + loc[:, 0:1] + loc[:, 2:3]
    part_ref[...] = jnp.where(lane == 0, one, jnp.where(lane == 1, two, 0.0))


def at(a):
    return pl.ds(pl.multiple_of(a * ROWS, ROWS), ROWS)


def weight(w_ref, a):
    pair = [jnp.broadcast_to(w_ref[part, pl.ds(a, 1), :], (ROWS, LANES)) for part in range(2)]
    return jnp.concatenate(pair * COLS, 1)


def narrow(v):
    return jnp.concatenate([v[:, c * TILE : c * TILE + LANES] for c in range(COLS)], 1)


def forward_kernel(
    x_ref, fwd_ref, w_ref, mid_ref, lift_ref, basis_ref, wave_ref, y_ref, ends_ref,
    xv, yb, in_sems, out_sems
):
    for t in range(STEPS):
        start_all(field_copies(x_ref, xv, in_sems, t))
    def loaded(a):
        return rows_at(xv, a) * PER_TURN

    def sources(start):
        u = loaded(jnp.maximum(start - 1, 0))
        here = loaded(start)
        above = turns(here - u)
        out, own = [], []
        for i in range(CHUNK):
            own.append(here)
            after = loaded(jnp.minimum(start + i + 1, TILE - 1))
            below = turns(after - here)
            out.append(below - above)
            here, above = after, below
        return [jnp.concatenate(v, 0).astype(jnp.bfloat16) for v in (out, own)]

    def wave(p, a):
        return wave_ref[p * (TILE // 2) + a]

    def gather_low(low, a, top, bottom):
        even, odd = top + bottom, top - bottom
        return (
            low[0] + even,
            low[1] + wave(1, a) * odd,
            low[2] + wave(2, a) * even,
            low[3] + wave(3, a) * odd,
        )

    def transform(t, low):
        top, own_top = sources(t * CHUNK)
        bottom, own_bottom = sources(TILE - CHUNK * (t + 1))
        stack = lambda u, v: jnp.concatenate([u[:, :TILE], u[:, TILE:], v[:, :TILE], v[:, TILE:]], 0)
        left = stack(own_top, own_bottom)
        both = jnp.dot(left, basis_ref[...], preferred_element_type=jnp.float32)
        kb, own = turns(both[:, :TILE]).astype(jnp.bfloat16), both[:, TILE:]
        piece = lambda k, i: own[(k * CHUNK + i) * ROWS : (k * CHUNK + i + 1) * ROWS]
        for i in range(CHUNK):
            pair = [
                jnp.concatenate([piece(2 * side, j), piece(2 * side + 1, j)], 1)
                for side, j in ((0, i), (1, CHUNK - 1 - i))
            ]
            low = gather_low(low, t * CHUNK + i, *pair)
        left = stack(top, bottom)
        left = jnp.concatenate([left, left, kb, kb], 1)
        y = jnp.dot(left, fwd_ref[...], preferred_element_type=jnp.float32)
        size = CHUNK * ROWS
        for side in range(2):
            start = (t * CHUNK if side == 0 else TILE - CHUNK * (t + 1)) * ROWS
            start = pl.multiple_of(start, size)
            for c in range(COLS):
                piece = y[(2 * side + c) * size : (2 * side + c + 1) * size]
                yb[pl.ds(start, size), c * TILE : (c + 1) * TILE] = piece
        return low

    def eliminate(t, carry):
        top, bottom, low = carry
        for i in range(CHUNK):
            a = t * CHUNK + i
            scale = weight(w_ref, jnp.maximum(a - 1, 0))
            own_top, own_bottom = yb[at(a), :], yb[at(TILE - 1 - a), :]
            low = gather_low(low, a, narrow(own_top), narrow(own_bottom))
            top = own_top + scale * top
            bottom = own_bottom + scale * bottom
            yb[at(a), :] = top
            yb[at(TILE - 1 - a), :] = bottom
        return top, bottom, low

    zero = jnp.zeros((ROWS, WIDTH), jnp.float32)
    none = (jnp.zeros((ROWS, COLS * LANES), jnp.float32),) * LOW
    for t in range(2):
        wait_all(field_copies(x_ref, xv, in_sems, t))
    low_z = transform(0, none)

    def forward(t, carry):
        carry, low_z = carry

        @pl.when(t + 1 < STEPS)
        def _():
            wait_all(field_copies(x_ref, xv, in_sems, t + 1))

        carry = eliminate(t - 1, carry)
        low_z = transform(t, low_z)
        start_all(row_copies(y_ref, yb, out_sems, t - 1, out=True))
        return carry, low_z

    carry, low_z = lax.fori_loop(1, STEPS, forward, ((zero, zero, none), low_z))
    top, bottom, low_y = eliminate(STEPS - 1, carry)
    start_all(row_copies(y_ref, yb, out_sems, STEPS - 1, out=True))
    lift = []
    for p in range(LOW):
        rows = [
            jnp.concatenate([lift_ref[k : k + 1, :]] * COLS, 1) for k in (p, LOW + p)
        ]
        lift.append(rows[0] * low_z[p] + rows[1] * low_y[p])
    lift[0] = lift[0] * (1.0 / TILE)
    even = mid_ref[0:1, :] * (top + bottom)
    odd = mid_ref[1:2, :] * (top - bottom)
    ends_ref[0:ROWS, :] = even + odd
    ends_ref[ROWS : 2 * ROWS, :] = even - odd
    for p in range(LOW):
        for c in range(COLS):
            ends_ref[(2 + p) * ROWS : (3 + p) * ROWS, c * TILE : c * TILE + LANES] = lift[p][
                :, c * LANES : (c + 1) * LANES
            ]
    for t in range(STEPS):
        wait_all(row_copies(y_ref, yb, out_sems, t, out=True))


def backward_kernel(
    x_ref, y_ref, ends_ref, bwd_ref, w_ref, wave_ref, p_ref, sum_ref,
    xv, yb, xb, x_sems, y_sems, out_sems
):
    for t in reversed(range(STEPS)):
        start_all(row_copies(y_ref, yb, y_sems, t))
        start_all(field_copies(x_ref, xv, x_sems, t))
    def wave(p, a):
        return wave_ref[p * (TILE // 2) + a]

    mid_top, mid_bottom = (ends_ref[k * ROWS : (k + 1) * ROWS, :] for k in range(2))
    lift = [narrow(ends_ref[(2 + p) * ROWS : (3 + p) * ROWS, :]) for p in range(LOW)]

    def substitute(t, carry):
        top, bottom, total = carry
        wait_all(row_copies(y_ref, yb, y_sems, t))
        for i in range(CHUNK):
            a = t * CHUNK + (CHUNK - 1 - i)
            scale = weight(w_ref, a)
            top = scale * (yb[at(a), :] + top)
            bottom = scale * (yb[at(TILE - 1 - a), :] + bottom)
            even = lift[0] + wave(2, a) * lift[2]
            odd = wave(1, a) * lift[1] + wave(3, a) * lift[3]
            for low, value, row in ((even + odd, top, a), (even - odd, bottom, TILE - 1 - a)):
                for part in range(PARTS):
                    piece = value[:, part * LANES : (part + 1) * LANES]
                    if part % 2 == 0:
                        piece = piece + low[:, part // 2 * LANES : (part // 2 + 1) * LANES]
                    xb[at(row), part * LANES : (part + 1) * LANES] = piece
            total = total + narrow(top + bottom)
        return top, bottom, total

    def restore(t):
        wait_all(field_copies(x_ref, xv, x_sems, t))
        size = CHUNK * ROWS
        pieces, starts = [], []
        for side in range(2):
            first = t * CHUNK if side == 0 else TILE - CHUNK * (t + 1)
            starts.append(first)
            block = xb[pl.ds(pl.multiple_of(first * ROWS, size), size), :]
            for c in range(COLS):
                pieces.append(block[:, c * TILE : (c + 1) * TILE])
        value = jnp.concatenate(pieces, 0)
        high = value.astype(jnp.bfloat16)
        low = (value - high.astype(jnp.float32)).astype(jnp.bfloat16)
        left = jnp.concatenate([high, low, high], 1)
        y = jnp.dot(left, bwd_ref[...], preferred_element_type=jnp.float32)
        for side in range(2):
            for i in range(CHUNK):
                where = pl.ds(starts[side] + i, ROWS, stride=PITCH)
                for part in range(PARTS):
                    from_row = (2 * side + part // 2) * size + i * ROWS
                    from_lane = (part % 2) * LANES
                    piece = y[from_row : from_row + ROWS, from_lane : from_lane + LANES]
                    xv[part, where, :] = xv[part, where, :] + piece
        start_all(field_copies(p_ref, xv, out_sems, t, out=True))

    carry = substitute(STEPS - 1, (mid_bottom, mid_top, jnp.zeros((ROWS, COLS * LANES), jnp.float32)))

    def backward(i, carry):
        t = STEPS - 2 - i
        carry = substitute(t, carry)
        restore(t + 1)
        return carry

    _, _, total = lax.fori_loop(0, STEPS - 1, backward, carry)
    restore(0)
    sum_ref[...] = total
    for t in range(STEPS):
        wait_all(field_copies(p_ref, xv, out_sems, t, out=True))


def finish_kernel(p_ref, sum_ref, part_ref, down_ref, out_ref, stage, in_sems, out_sems):
    def block(row, out):
        rows = stage.at[row]
        ends = (rows, out_ref.at[row]) if out else (p_ref.at[row], rows)
        return pltpu.make_async_copy(*ends, (out_sems if out else in_sems).at[row])

    for row in range(ROWS):
        block(row, False).start()
    me = lax.axis_index("row")
    peers = down_ref.shape[0]
    before = jnp.zeros((1, 1), jnp.float32)
    for peer in range(peers - 1):
        border = turns((down_ref[peer + 1, 0:2, :] - down_ref[peer, 2:4, :]) * PER_TURN)
        border = jnp.sum(jnp.sum(border, axis=1, keepdims=True), axis=0, keepdims=True)
        both = border * (1.0 / TILE) + down_ref[peer, 4:5, 0:1]
        before = before + jnp.where(peer < me, both, 0.0)
    shared = before - down_ref[0, 4:5, 1:2]
    mean = down_ref[0, 4:5, 2:3]
    shift = []
    for c in range(COLS):
        level = sum_ref[:, c * LANES : c * LANES + 1] * (1.0 / (16.0 * TILE))
        value = -mean - TURN * (part_ref[:, c : c + 1] + shared + level)
        shift.append(jnp.broadcast_to(value, (ROWS, LANES)))
    shift = jnp.concatenate([shift[part // 2] for part in range(PARTS)], 1)
    for row in range(ROWS):
        block(row, False).wait()
        stage[row] = stage[row] + shift[row : row + 1, :]
        block(row, True).start()
    for row in range(ROWS):
        block(row, True).wait()


VMEM = pl.BlockSpec(memory_space=pltpu.VMEM)
HBM = pl.BlockSpec(memory_space=pltpu.HBM)
FIELD = pltpu.VMEM((PARTS, ROWS * PITCH, LANES), jnp.float32)
SMEM = pl.BlockSpec(memory_space=pltpu.SMEM)


def f32(*shape):
    return jax.ShapeDtypeStruct(shape, jnp.float32)


def in_hbm(x):
    return pltpu.with_memory_space_constraint(x, pltpu.HBM)


def to_all(x, axis):
    return lax.all_to_all(x, axis, 0, 0, tiled=True)


def per_device(phase):
    *big, low = tables()
    forward, backward, weights, middle = (jnp.asarray(t) for t in big)
    low = {k: jnp.asarray(v) for k, v in low.items()}
    grid = in_hbm(phase.reshape(ROWS, TILE, WIDTH))
    peers = {axis: lax.axis_size(axis) for axis in ("row", "col")}
    msg, loc = pl.pallas_call(
        counts_kernel,
        out_shape=(
            f32(peers["col"], MSG, LANES),
            f32(ROWS, LANES),
        ),
        in_specs=[HBM] * 4,
        out_specs=(VMEM,) * 2,
        scratch_shapes=[
            pltpu.VMEM((MSG, LANES), jnp.float32),
            FIELD,
            pltpu.VMEM((8, TILE), jnp.float32),
            pltpu.SMEM((4 * TILE,), jnp.float32),
            pltpu.VMEM((TILE, TILE), jnp.bfloat16),
            pltpu.SemaphoreType.DMA((LOADS * PARTS,)),
            pltpu.SemaphoreType.DMA((3,)),
        ],
        compiler_params=pltpu.CompilerParams(vmem_limit_bytes=8 << 20),
        cost_estimate=pl.CostEstimate(flops=1 << 30, bytes_accessed=4 << 20, transcendentals=0),
        name="counts",
    )(grid, in_hbm(low["edges"]), in_hbm(low["steps"]), in_hbm(low["across"]))
    got = to_all(msg, "col")
    yb, ends = pl.pallas_call(
        forward_kernel,
        out_shape=(pltpu.HBM((ROWS * TILE, WIDTH), jnp.float32), f32((2 + LOW) * ROWS, WIDTH)),
        in_specs=[HBM] + [VMEM] * 5 + [SMEM],
        out_specs=(HBM, VMEM),
        scratch_shapes=[
            pltpu.VMEM((PARTS, ROWS * PITCH, LANES), jnp.float32),
            pltpu.VMEM((ROWS * TILE, WIDTH), jnp.float32),
            pltpu.SemaphoreType.DMA((2 * STEPS * PARTS,)),
            pltpu.SemaphoreType.DMA((2 * STEPS,)),
        ],
        compiler_params=pltpu.CompilerParams(vmem_limit_bytes=12 << 20),
        cost_estimate=pl.CostEstimate(flops=8 << 30, bytes_accessed=8 << 20, transcendentals=0),
        name="ahead",
    )(grid, forward, weights, middle, low["lift"], low["basis"], low["waves"])
    down, part = pl.pallas_call(
        across_kernel,
        out_shape=(f32(peers["row"], ROWS, LANES), f32(ROWS, LANES)),
        in_specs=[VMEM, VMEM],
        out_specs=(VMEM, VMEM),
        compiler_params=pltpu.CompilerParams(vmem_limit_bytes=4 << 20),
        name="across",
    )(got, loc)
    downs = to_all(down, "row")
    p, total = pl.pallas_call(
        backward_kernel,
        out_shape=(pltpu.HBM((ROWS, TILE, WIDTH), jnp.float32), f32(ROWS, COLS * LANES)),
        in_specs=[HBM, HBM] + [VMEM] * 3 + [SMEM],
        out_specs=(HBM, VMEM),
        scratch_shapes=[
            pltpu.VMEM((PARTS, ROWS * PITCH, LANES), jnp.float32),
            pltpu.VMEM((ROWS * TILE, WIDTH), jnp.float32),
            pltpu.VMEM((ROWS * TILE, WIDTH), jnp.float32),
            pltpu.SemaphoreType.DMA((2 * STEPS * PARTS,)),
            pltpu.SemaphoreType.DMA((2 * STEPS,)),
            pltpu.SemaphoreType.DMA((2 * STEPS * PARTS,)),
        ],
        compiler_params=pltpu.CompilerParams(vmem_limit_bytes=16 << 20),
        cost_estimate=pl.CostEstimate(flops=8 << 30, bytes_accessed=8 << 20, transcendentals=0),
        name="back",
    )(grid, in_hbm(yb), ends, backward, weights, low["waves"])
    out = pl.pallas_call(
        finish_kernel,
        out_shape=f32(ROWS, TILE, WIDTH),
        in_specs=[HBM, VMEM, VMEM, VMEM],
        out_specs=HBM,
        scratch_shapes=[
            pltpu.VMEM((ROWS, TILE, WIDTH), jnp.float32),
            pltpu.SemaphoreType.DMA((ROWS,)),
            pltpu.SemaphoreType.DMA((ROWS,)),
        ],
        compiler_params=pltpu.CompilerParams(vmem_limit_bytes=8 << 20),
        name="finish",
    )(in_hbm(p), total, part, downs)
    return out.reshape(phase.shape)


def solution(mesh):
    return jax.shard_map(
        per_device, mesh=mesh, in_specs=(P("row", "col"),), out_specs=P("row", "col"), check_vma=False
    )
```

time: 68.5 us -> 46 us (0.67)
  blocking collectives: 15.8 us -> 0 us
  local copies, waits for them, and re-layouts: 7.57 us -> 0.04 us
  starting transfers between devices: 11 us -> 18.1 us
  Pallas kernels: 33.7 us -> 27.4 us
    all_to_all x1 -> x0, blocking collectives: 15.8 us -> none  [to_all(): lax.all_to_all(jnp.broadcast_to(x[None], (peers, *x.shape)), axis, 0, 0,...]
    all_to_all x1 -> x2, starting transfers between devices: 11 us -> 18.1 us  [to_all(): return lax.all_to_all(x, axis, 0, 0, tiled=True)]
    pallas_call x4 -> x5, Pallas kernels: 33.7 us -> 27.4 us  [the longest x1 8.91 us: per_device(): pl.pallas_call(backward_kernel, out_shape=(pltpu.HBM((ROWS, TILE, WIDTH),...]
    unnamed x26 -> x14, local copies, waits for them, and re-layouts: 6.23 us -> 0.04 us
    broadcast_in_dim x2 -> x0, local copies, waits for them, and re-layouts: 1.34 us -> none  [to_all(): jnp.broadcast_to(x[None], (peers, *x.shape))]
  transfers between devices with their start and end apart: 1 -> 2, of which waited for: 0 -> 0; matrix products, arithmetic and copies ran while one was open for 0% -> 0% of each run, Pallas kernels for 32% -> 38%
where the time goes in v1:
time: 46 us; the launch traced here: 45.7 us
  Pallas kernels  27.4 us (60%)
  starting transfers between devices  18.1 us (39%)
    all_to_all x2, starting transfers between devices, to_all(): return lax.all_to_all(x, axis, 0, 0, tiled=True)  18.1 us
    pallas_call x1, Pallas kernels, per_device(): pl.pallas_call(backward_kernel, out_shape=(pltpu.HBM((ROWS, TILE, WIDTH),...  8.91 us
    pallas_call x1, Pallas kernels, per_device(): pl.pallas_call(forward_kernel, out_shape=(pltpu.HBM((ROWS * TILE, WIDTH),...  8.66 us
    pallas_call x1, Pallas kernels, per_device(): pl.pallas_call(counts_kernel, out_shape=(f32(peers['col'], MSG, LANES), f...  5.43 us
    pallas_call x1, Pallas kernels, per_device(): pl.pallas_call(finish_kernel, out_shape=f32(ROWS, TILE, WIDTH), in_specs=...  3.66 us
  transfers between devices with their start and end apart: 2, of which 0 were waited for; matrix products, arithmetic and copies ran while one was open for 0% of the time, Pallas kernels for 38%

profile of v1, /device:TPU:1, one launch (start us, length us, event | category | flops | bytes accessed | tf_op | source)
XLA Modules:
  0.0 45.7 jit_solution(1616996028228321163)
XLA Ops:
  0.0 0.0 copy-start
  0.0 0.0 copy-start.3
  0.0 0.0 copy-start.4
  0.0 0.0 copy-start.5
  0.0 0.0 copy-start.2
  0.0 0.0 copy-start.6
  0.0 5.4 %counts.1 = (f32[16,48,128]{2,1,0:T(8,128)}, f32[8,128]{1,0:T(8,128)S(1)}) custom-call(f32[8,256,512]{2,1,0:T(8,128)} %bitcast.2, f32[8,256]{1,0:T(8,128)} %constant.28.clone.edge_hbm, f32[1024]{0:T(1024)} %constant.29.clone.step_hbm, bf16[256,256]{1,0:T(8,128)(2,1)} %constant.26.clone.across_hbm), custom_call_target="tpu_custom_call" | custom-call | flops 1073741824 | bytes 4194304 | tf_op jit(solution)/shard_map/counts/pallas_call | solution.py:554
  5.5 7.6 %all-to-all-start = ((f32[16,48,128]{2,1,0:T(8,128)}), f32[16,48,128]{2,1,0:T(8,128)S(1)}, u32[]{:S(2)}, u32[]{:S(2)}) async-start(f32[16,48,128]{2,1,0:T(8,128)} %get-tuple-element.17), calls=%async_computation | async-start | bytes 786432 | tf_op jit(solution)/shard_map/all_to_all | solution.py:545
  13.1 0.0 copy-done
  13.1 0.0 copy-done.3
  13.1 0.0 copy-done.4
  13.1 0.0 copy-done.5
  13.1 0.0 copy-done.2
  13.1 0.0 copy-done.6
  13.1 0.0 copy-start.1
  13.2 8.7 %ahead.1 = (f32[2048,512]{1,0:T(8,128)}, f32[48,512]{1,0:T(8,128)S(1)}) custom-call(f32[8,256,512]{2,1,0:T(8,128)} %bitcast.3, bf16[1024,256]{1,0:T(8,128)(2,1)S(1)} %copy-done, f32[2,128,128]{2,1,0:T(8,128)S(1)} %copy-done.3, f32[2,512]{1,0:T(2,128)S(1)} %copy-done.4, f32[8,128]{1,0:T(8,128)S(1)} %copy-done.5, bf16[256,384]{1,0:T(8,128)(2,1)S(1)} %copy-done.2, ...), custom_call_target="tpu_custom_call" | custom-call | flops 8589934592 | bytes 8388608 | tf_op jit(solution)/shard_map/ahead/pallas_call | solution.py:576
  21.8 0.0 all-to-all-done.got_ref
  21.8 0.8 %across.1 = (f32[16,8,128]{2,1,0:T(8,128)}, f32[8,128]{1,0:T(8,128)S(1)}) custom-call(f32[16,48,128]{2,1,0:T(8,128)S(1)} %all-to-all-done.got_ref, f32[8,128]{1,0:T(8,128)S(1)} %get-tuple-element.18.loc_ref), custom_call_target="tpu_custom_call" | custom-call | tf_op jit(solution)/shard_map/across/pallas_call | solution.py:591
  22.6 10.5 %all-to-all-start.1 = ((f32[16,8,128]{2,1,0:T(8,128)}), f32[16,8,128]{2,1,0:T(8,128)S(1)}, u32[]{:S(2)}, u32[]{:S(2)}) async-start(f32[16,8,128]{2,1,0:T(8,128)} %get-tuple-element.20), calls=%async_computation.1 | async-start | bytes 131072 | tf_op jit(solution)/shard_map/all_to_all | solution.py:545
  33.1 0.0 copy-done.1
  33.1 8.9 %back.1 = (f32[8,256,512]{2,1,0:T(8,128)}, f32[8,256]{1,0:T(8,128)S(1)}) custom-call(f32[8,256,512]{2,1,0:T(8,128)} %bitcast.4, f32[2048,512]{1,0:T(8,128)} %get-tuple-element.13.y_ref, f32[48,512]{1,0:T(8,128)S(1)} %get-tuple-element.14.ends_ref, bf16[768,256]{1,0:T(8,128)(2,1)S(1)} %copy-done.1, f32[2,128,128]{2,1,0:T(8,128)S(1)} %copy-done.3, ...), custom_call_target="tpu_custom_call" | custom-call | flops 8589934592 | bytes 8388608 | tf_op jit(solution)/shard_map/back/pallas_call | solution.py:600
  42.0 0.0 all-to-all-done.1.down_ref
  42.1 3.7 %finish.1 = f32[8,256,512]{2,1,0:T(8,128)} custom-call(f32[8,256,512]{2,1,0:T(8,128)} %get-tuple-element.15.p_ref, f32[8,256]{1,0:T(8,128)S(1)} %get-tuple-element.16.sum_ref, f32[8,128]{1,0:T(8,128)S(1)} %get-tuple-element.19.part_ref, f32[16,8,128]{2,1,0:T(8,128)S(1)} %all-to-all-done.1.down_ref), custom_call_target="tpu_custom_call" | custom-call | tf_op jit(solution)/shard_map/finish/pallas_call | solution.py:617
Async XLA Ops:
  0.0 13.1 %copy-start = (bf16[1024,256]{1,0:T(8,128)(2,1)S(1)}, bf16[1024,256]{1,0:T(8,128)(2,1)}, u32[]{:S(2)}) copy-start(bf16[1024,256]{1,0:T(8,128)(2,1)} %constant.20.clone.fwd_ref) | copy-start | bytes 1572868
  0.0 13.1 %copy-start.3 = (f32[2,128,128]{2,1,0:T(8,128)S(1)}, f32[2,128,128]{2,1,0:T(8,128)}, u32[]{:S(2)}) copy-start(f32[2,128,128]{2,1,0:T(8,128)} %constant.22.clone.w_ref) | copy-start | bytes 393220
  0.0 13.1 %copy-start.4 = (f32[2,512]{1,0:T(2,128)S(1)}, f32[2,512]{1,0:T(2,128)}, u32[]{:S(2)}) copy-start(f32[2,512]{1,0:T(2,128)} %constant.23.clone.mid_ref) | copy-start | bytes 12292
  0.0 13.1 %copy-start.5 = (f32[8,128]{1,0:T(8,128)S(1)}, f32[8,128]{1,0:T(8,128)}, u32[]{:S(2)}) copy-start(f32[8,128]{1,0:T(8,128)} %constant.24.clone.lift_ref) | copy-start | bytes 12292
  0.0 13.1 %copy-start.2 = (bf16[256,384]{1,0:T(8,128)(2,1)S(1)}, bf16[256,384]{1,0:T(8,128)(2,1)}, u32[]{:S(2)}) copy-start(bf16[256,384]{1,0:T(8,128)(2,1)} %constant.25.clone.basis_ref) | copy-start | bytes 589828
  0.0 13.1 %copy-start.6 = (f32[512]{0:T(512)S(1)}, f32[512]{0:T(512)}, u32[]{:S(2)}) copy-start(f32[512]{0:T(512)} %constant.27.clone.wave_ref) | copy-start | bytes 6148
  5.5 16.3 %all-to-all-start = ((f32[16,48,128]{2,1,0:T(8,128)}), f32[16,48,128]{2,1,0:T(8,128)S(1)}, u32[]{:S(2)}, u32[]{:S(2)}) async-start(f32[16,48,128]{2,1,0:T(8,128)} %get-tuple-element.17), calls=%async_computation | async-start | bytes 786432 | tf_op jit(solution)/shard_map/all_to_all | solution.py:545
  13.1 20.0 %copy-start.1 = (bf16[768,256]{1,0:T(8,128)(2,1)S(1)}, bf16[768,256]{1,0:T(8,128)(2,1)}, u32[]{:S(2)}) copy-start(bf16[768,256]{1,0:T(8,128)(2,1)} %constant.21.clone.bwd_ref) | copy-start | bytes 1179652
  22.6 19.4 %all-to-all-start.1 = ((f32[16,8,128]{2,1,0:T(8,128)}), f32[16,8,128]{2,1,0:T(8,128)S(1)}, u32[]{:S(2)}, u32[]{:S(2)}) async-start(f32[16,8,128]{2,1,0:T(8,128)} %get-tuple-element.20), calls=%async_computation.1 | async-start | bytes 131072 | tf_op jit(solution)/shard_map/all_to_all | solution.py:545

commit v2 on v1

--- a/solution.py
+++ b/solution.py
@@ -19,6 +19,9 @@
 LANES = 128
 PARTS = WIDTH // LANES
 PITCH = TILE + 8
+SUB = 8
+BLOCKS = TILE // SUB * PARTS
+BLOCK_PITCH = BLOCKS + 1
 LOADS = 8
 CHUNK = 16
 STEPS = TILE // (2 * CHUNK)
@@ -129,6 +132,25 @@
     return copies
 
 
+def span_copy(x_ref, xv, sem, start, size, out=False):
+    first = start * PARTS // SUB if isinstance(start, int) else start // SUB * PARTS
+    blocks = pl.ds(first, size * PARTS // SUB)
+    ends = (x_ref.at[:, blocks], xv.at[:, blocks])
+    return pltpu.make_async_copy(*(ends[::-1] if out else ends), sem)
+
+
+def block_copies(x_ref, xv, sems, t, out=False):
+    return [
+        span_copy(x_ref, xv, sems.at[2 * t + side], side_start(t, side), CHUNK, out)
+        for side in range(2)
+    ]
+
+
+def row_set(xv, base, i, part):
+    start = base * PARTS + (i // SUB * PARTS + part) * SUB + i % SUB
+    return xv.reshape(ROWS * BLOCK_PITCH * SUB, LANES), pl.ds(start, ROWS, stride=BLOCK_PITCH * SUB)
+
+
 def row_copies(y_ref, yb, sems, t, out=False):
     copies = []
     for side in range(2):
@@ -425,20 +447,19 @@
 
 def backward_kernel(
     x_ref, y_ref, ends_ref, bwd_ref, w_ref, wave_ref, p_ref, sum_ref,
-    xv, yb, xb, x_sems, y_sems, out_sems
+    xv, yb, pv, even_ref, odd_ref, x_sems, y_sems, out_sems
 ):
     for t in reversed(range(STEPS)):
         start_all(row_copies(y_ref, yb, y_sems, t))
-        start_all(field_copies(x_ref, xv, x_sems, t))
+        start_all(block_copies(x_ref, xv, x_sems, t))
     def wave(p, a):
         return wave_ref[p * (TILE // 2) + a]
 
     mid_top, mid_bottom = (ends_ref[k * ROWS : (k + 1) * ROWS, :] for k in range(2))
     lift = [narrow(ends_ref[(2 + p) * ROWS : (3 + p) * ROWS, :]) for p in range(LOW)]
 
-    def substitute(t, carry):
+    def substitute(t, carry, to_ref):
         top, bottom, total = carry
-        wait_all(row_copies(y_ref, yb, y_sems, t))
         for i in range(CHUNK):
             a = t * CHUNK + (CHUNK - 1 - i)
             scale = weight(w_ref, a)
@@ -446,25 +467,24 @@
             bottom = scale * (yb[at(TILE - 1 - a), :] + bottom)
             even = lift[0] + wave(2, a) * lift[2]
             odd = wave(1, a) * lift[1] + wave(3, a) * lift[3]
-            for low, value, row in ((even + odd, top, a), (even - odd, bottom, TILE - 1 - a)):
+            for low, value, row in ((even + odd, top, CHUNK - 1 - i), (even - odd, bottom, CHUNK + i)):
                 for part in range(PARTS):
                     piece = value[:, part * LANES : (part + 1) * LANES]
                     if part % 2 == 0:
                         piece = piece + low[:, part // 2 * LANES : (part // 2 + 1) * LANES]
-                    xb[at(row), part * LANES : (part + 1) * LANES] = piece
+                    rows = slice(row * ROWS, (row + 1) * ROWS)
+                    to_ref[rows, part * LANES : (part + 1) * LANES] = piece
             total = total + narrow(top + bottom)
         return top, bottom, total
 
-    def restore(t):
-        wait_all(field_copies(x_ref, xv, x_sems, t))
+    def restore(t, from_ref):
         size = CHUNK * ROWS
         pieces, starts = [], []
         for side in range(2):
-            first = t * CHUNK if side == 0 else TILE - CHUNK * (t + 1)
-            starts.append(first)
-            block = xb[pl.ds(pl.multiple_of(first * ROWS, size), size), :]
+            starts.append(t * CHUNK if side == 0 else TILE - CHUNK * (t + 1))
             for c in range(COLS):
-                pieces.append(block[:, c * TILE : (c + 1) * TILE])
+                rows = slice(side * size, (side + 1) * size)
+                pieces.append(from_ref[rows, c * TILE : (c + 1) * TILE])
         value = jnp.concatenate(pieces, 0)
         high = value.astype(jnp.bfloat16)
         low = (value - high.astype(jnp.float32)).astype(jnp.bfloat16)
@@ -472,27 +492,40 @@
         y = jnp.dot(left, bwd_ref[...], preferred_element_type=jnp.float32)
         for side in range(2):
             for i in range(CHUNK):
-                where = pl.ds(starts[side] + i, ROWS, stride=PITCH)
                 for part in range(PARTS):
                     from_row = (2 * side + part // 2) * size + i * ROWS
                     from_lane = (part % 2) * LANES
                     piece = y[from_row : from_row + ROWS, from_lane : from_lane + LANES]
-                    xv[part, where, :] = xv[part, where, :] + piece
-        start_all(field_copies(p_ref, xv, out_sems, t, out=True))
-
-    carry = substitute(STEPS - 1, (mid_bottom, mid_top, jnp.zeros((ROWS, COLS * LANES), jnp.float32)))
-
-    def backward(i, carry):
-        t = STEPS - 2 - i
-        carry = substitute(t, carry)
-        restore(t + 1)
+                    flat, rows = row_set(xv, starts[side], i, part)
+                    moved, _ = row_set(pv, starts[side], i, part)
+                    moved[rows, :] = flat[rows, :] + piece
+
+    odd_ref[...] = jnp.zeros(odd_ref.shape, jnp.float32)
+
+    def backward(j, carry):
+        t = STEPS - 1 - 2 * j
+        for k in range(2):
+            wait_all(row_copies(y_ref, yb, y_sems, t - k))
+            wait_all(block_copies(x_ref, xv, x_sems, t - k))
+        carry = substitute(t, carry, even_ref)
+        restore(jnp.minimum(t + 1, STEPS - 1), odd_ref)
+        carry = substitute(t - 1, carry, odd_ref)
+        restore(t, even_ref)
+
+        @pl.when(j > 0)
+        def _():
+            start_all(block_copies(p_ref, pv, out_sems, t + 1, out=True))
+
+        start_all(block_copies(p_ref, pv, out_sems, t, out=True))
         return carry
 
-    _, _, total = lax.fori_loop(0, STEPS - 1, backward, carry)
-    restore(0)
+    begin = (mid_bottom, mid_top, jnp.zeros((ROWS, COLS * LANES), jnp.float32))
+    _, _, total = lax.fori_loop(0, STEPS // 2, backward, begin)
+    restore(0, odd_ref)
+    start_all(block_copies(p_ref, pv, out_sems, 0, out=True))
     sum_ref[...] = total
     for t in range(STEPS):
-        wait_all(field_copies(p_ref, xv, out_sems, t, out=True))
+        wait_all(block_copies(p_ref, pv, out_sems, t, out=True))
 
 
 def finish_kernel(p_ref, sum_ref, part_ref, down_ref, out_ref, stage, in_sems, out_sems):
@@ -518,10 +551,11 @@
         level = sum_ref[:, c * LANES : c * LANES + 1] * (1.0 / (16.0 * TILE))
         value = -mean - TURN * (part_ref[:, c : c + 1] + shared + level)
         shift.append(jnp.broadcast_to(value, (ROWS, LANES)))
-    shift = jnp.concatenate([shift[part // 2] for part in range(PARTS)], 1)
     for row in range(ROWS):
         block(row, False).wait()
-        stage[row] = stage[row] + shift[row : row + 1, :]
+        for part in range(PARTS):
+            view = stage.reshape(ROWS, BLOCKS // PARTS, PARTS, SUB, LANES).at[row, :, part]
+            view[...] = view[...] + shift[part // 2][row : row + 1, :][None]
         block(row, True).start()
     for row in range(ROWS):
         block(row, True).wait()
@@ -529,6 +563,8 @@
 
 VMEM = pl.BlockSpec(memory_space=pltpu.VMEM)
 HBM = pl.BlockSpec(memory_space=pltpu.HBM)
+PIECE = pltpu.VMEM((2 * CHUNK * ROWS, WIDTH), jnp.float32)
+BLOCK_FIELD = pltpu.VMEM((ROWS, BLOCK_PITCH, SUB, LANES), jnp.float32)
 FIELD = pltpu.VMEM((PARTS, ROWS * PITCH, LANES), jnp.float32)
 SMEM = pl.BlockSpec(memory_space=pltpu.SMEM)
 
@@ -549,6 +585,8 @@
     *big, low = tables()
     forward, backward, weights, middle = (jnp.asarray(t) for t in big)
     low = {k: jnp.asarray(v) for k, v in low.items()}
+    blocks = phase.reshape(ROWS, TILE // SUB, SUB, PARTS, LANES).swapaxes(2, 3)
+    blocks = blocks.reshape(ROWS, BLOCKS, SUB, LANES)
     grid = in_hbm(phase.reshape(ROWS, TILE, WIDTH))
     peers = {axis: lax.axis_size(axis) for axis in ("row", "col")}
     msg, loc = pl.pallas_call(
@@ -599,35 +637,38 @@
     downs = to_all(down, "row")
     p, total = pl.pallas_call(
         backward_kernel,
-        out_shape=(pltpu.HBM((ROWS, TILE, WIDTH), jnp.float32), f32(ROWS, COLS * LANES)),
+        out_shape=(pltpu.HBM((ROWS, BLOCKS, SUB, LANES), jnp.float32), f32(ROWS, COLS * LANES)),
         in_specs=[HBM, HBM] + [VMEM] * 3 + [SMEM],
         out_specs=(HBM, VMEM),
         scratch_shapes=[
-            pltpu.VMEM((PARTS, ROWS * PITCH, LANES), jnp.float32),
+            BLOCK_FIELD,
             pltpu.VMEM((ROWS * TILE, WIDTH), jnp.float32),
-            pltpu.VMEM((ROWS * TILE, WIDTH), jnp.float32),
-            pltpu.SemaphoreType.DMA((2 * STEPS * PARTS,)),
+            BLOCK_FIELD,
+            PIECE,
+            PIECE,
             pltpu.SemaphoreType.DMA((2 * STEPS,)),
-            pltpu.SemaphoreType.DMA((2 * STEPS * PARTS,)),
+            pltpu.SemaphoreType.DMA((2 * STEPS,)),
+            pltpu.SemaphoreType.DMA((2 * STEPS,)),
         ],
-        compiler_params=pltpu.CompilerParams(vmem_limit_bytes=16 << 20),
+        compiler_params=pltpu.CompilerParams(vmem_limit_bytes=24 << 20),
         cost_estimate=pl.CostEstimate(flops=8 << 30, bytes_accessed=8 << 20, transcendentals=0),
         name="back",
-    )(grid, in_hbm(yb), ends, backward, weights, low["waves"])
+    )(in_hbm(blocks), in_hbm(yb), ends, backward, weights, low["waves"])
     out = pl.pallas_call(
         finish_kernel,
-        out_shape=f32(ROWS, TILE, WIDTH),
+        out_shape=f32(ROWS, BLOCKS, SUB, LANES),
         in_specs=[HBM, VMEM, VMEM, VMEM],
         out_specs=HBM,
         scratch_shapes=[
-            pltpu.VMEM((ROWS, TILE, WIDTH), jnp.float32),
+            pltpu.VMEM((ROWS, BLOCKS, SUB, LANES), jnp.float32),
             pltpu.SemaphoreType.DMA((ROWS,)),
             pltpu.SemaphoreType.DMA((ROWS,)),
         ],
         compiler_params=pltpu.CompilerParams(vmem_limit_bytes=8 << 20),
         name="finish",
     )(in_hbm(p), total, part, downs)
-    return out.reshape(phase.shape)
+    blocks = out.reshape(ROWS, TILE // SUB, PARTS, SUB, LANES).swapaxes(2, 3)
+    return blocks.reshape(phase.shape)
 
 
 def solution(mesh):

time: 46 us -> 44.6 us (0.970)
  Pallas kernels: 27.4 us -> 25.9 us
    pallas_call x2, Pallas kernels: 12.6 us -> 11 us  [the longest x1 7.66 us: per_device(): pl.pallas_call(backward_kernel, out_shape=(pltpu.HBM((ROWS, BLOCKS, SUB,...]
  transfers between devices with their start and end apart: 2 -> 2, of which waited for: 0 -> 1; matrix products, arithmetic and copies ran while one was open for 0% -> 0% of each run, Pallas kernels for 38% -> 37%
where the time goes in v2:
time: 44.6 us; the launch traced here: 44.3 us
  Pallas kernels  25.9 us (58%)
  starting transfers between devices  18.1 us (41%)
    all_to_all x2, starting transfers between devices, to_all(): return lax.all_to_all(x, axis, 0, 0, tiled=True)  18.1 us
    pallas_call x1, Pallas kernels, per_device(): pl.pallas_call(forward_kernel, out_shape=(pltpu.HBM((ROWS * TILE, WIDTH),...  8.66 us
    pallas_call x1, Pallas kernels, per_device(): pl.pallas_call(backward_kernel, out_shape=(pltpu.HBM((ROWS, BLOCKS, SUB,...  7.66 us
    pallas_call x1, Pallas kernels, per_device(): pl.pallas_call(counts_kernel, out_shape=(f32(peers['col'], MSG, LANES), f...  5.43 us
    pallas_call x1, Pallas kernels, per_device(): pl.pallas_call(finish_kernel, out_shape=f32(ROWS, BLOCKS, SUB, LANES), in...  3.39 us
  transfers between devices with their start and end apart: 2, of which 1 were waited for; matrix products, arithmetic and copies ran while one was open for 0% of the time, Pallas kernels for 37%

profile of v2, /device:TPU:1, one launch (start us, length us, event | category | flops | bytes accessed | tf_op | source)
XLA Modules:
  0.0 44.3 jit_solution(17154686375052490137)
XLA Ops:
  0.0 0.0 copy-start
  0.0 0.0 copy-start.3
  0.0 0.0 copy-start.4
  0.0 0.0 copy-start.5
  0.0 0.0 copy-start.2
  0.0 0.0 copy-start.6
  0.0 5.4 %counts.1 = (f32[16,48,128]{2,1,0:T(8,128)}, f32[8,128]{1,0:T(8,128)S(1)}) custom-call(f32[8,256,512]{2,1,0:T(8,128)} %bitcast.11, f32[8,256]{1,0:T(8,128)} %constant.28.clone.edge_hbm, f32[1024]{0:T(1024)} %constant.29.clone.step_hbm, bf16[256,256]{1,0:T(8,128)(2,1)} %constant.26.clone.across_hbm), custom_call_target="tpu_custom_call" | custom-call | flops 1073741824 | bytes 4194304 | tf_op jit(solution)/shard_map/counts/pallas_call | solution.py:592
  5.5 7.6 %all-to-all-start = ((f32[16,48,128]{2,1,0:T(8,128)}), f32[16,48,128]{2,1,0:T(8,128)S(1)}, u32[]{:S(2)}, u32[]{:S(2)}) async-start(f32[16,48,128]{2,1,0:T(8,128)} %get-tuple-element.17), calls=%async_computation | async-start | bytes 786432 | tf_op jit(solution)/shard_map/all_to_all | solution.py:581
  13.1 0.0 copy-done
  13.1 0.0 copy-done.3
  13.1 0.0 copy-done.4
  13.1 0.0 copy-done.5
  13.1 0.0 copy-done.2
  13.1 0.0 copy-done.6
  13.1 0.0 copy-start.1
  13.2 8.7 %ahead.1 = (f32[2048,512]{1,0:T(8,128)}, f32[48,512]{1,0:T(8,128)S(1)}) custom-call(f32[8,256,512]{2,1,0:T(8,128)} %bitcast.12, bf16[1024,256]{1,0:T(8,128)(2,1)S(1)} %copy-done, f32[2,128,128]{2,1,0:T(8,128)S(1)} %copy-done.3, f32[2,512]{1,0:T(2,128)S(1)} %copy-done.4, f32[8,128]{1,0:T(8,128)S(1)} %copy-done.5, bf16[256,384]{1,0:T(8,128)(2,1)S(1)} %copy-done.2, ...), custom_call_target="tpu_custom_call" | custom-call | flops 8589934592 | bytes 8388608 | tf_op jit(solution)/shard_map/ahead/pallas_call | solution.py:614
  21.8 0.0 all-to-all-done.got_ref
  21.8 0.8 %across.1 = (f32[16,8,128]{2,1,0:T(8,128)}, f32[8,128]{1,0:T(8,128)S(1)}) custom-call(f32[16,48,128]{2,1,0:T(8,128)S(1)} %all-to-all-done.got_ref, f32[8,128]{1,0:T(8,128)S(1)} %get-tuple-element.18.loc_ref), custom_call_target="tpu_custom_call" | custom-call | tf_op jit(solution)/shard_map/across/pallas_call | solution.py:629
  22.6 10.5 %all-to-all-start.1 = ((f32[16,8,128]{2,1,0:T(8,128)}), f32[16,8,128]{2,1,0:T(8,128)S(1)}, u32[]{:S(2)}, u32[]{:S(2)}) async-start(f32[16,8,128]{2,1,0:T(8,128)} %get-tuple-element.20), calls=%async_computation.1 | async-start | bytes 131072 | tf_op jit(solution)/shard_map/all_to_all | solution.py:581
  33.1 0.0 copy-done.1
  33.1 7.7 %back.1 = (f32[8,128,8,128]{3,2,1,0:T(8,128)}, f32[8,256]{1,0:T(8,128)S(1)}) custom-call(f32[8,128,8,128]{3,2,1,0:T(8,128)} %bitcast.13, f32[2048,512]{1,0:T(8,128)} %get-tuple-element.13.y_ref, f32[48,512]{1,0:T(8,128)S(1)} %get-tuple-element.14.ends_ref, bf16[768,256]{1,0:T(8,128)(2,1)S(1)} %copy-done.1, f32[2,128,128]{2,1,0:T(8,128)S(1)} %copy-done.3, ...), custom_call_target="tpu_custom_call" | custom-call | flops 8589934592 | bytes 8388608 | tf_op jit(solution)/shard_map/back/pallas_call | solution.py:638
  40.8 0.1 all-to-all-done.1.down_ref
  40.9 3.4 %finish.1 = f32[8,128,8,128]{3,2,1,0:T(8,128)} custom-call(f32[8,128,8,128]{3,2,1,0:T(8,128)} %get-tuple-element.15.p_ref, f32[8,256]{1,0:T(8,128)S(1)} %get-tuple-element.16.sum_ref, f32[8,128]{1,0:T(8,128)S(1)} %get-tuple-element.19.part_ref, f32[16,8,128]{2,1,0:T(8,128)S(1)} %all-to-all-done.1.down_ref), custom_call_target="tpu_custom_call" | custom-call | tf_op jit(solution)/shard_map/finish/pallas_call | solution.py:657
Async XLA Ops:
  0.0 13.1 %copy-start = (bf16[1024,256]{1,0:T(8,128)(2,1)S(1)}, bf16[1024,256]{1,0:T(8,128)(2,1)}, u32[]{:S(2)}) copy-start(bf16[1024,256]{1,0:T(8,128)(2,1)} %constant.20.clone.fwd_ref) | copy-start | bytes 1572868
  0.0 13.1 %copy-start.3 = (f32[2,128,128]{2,1,0:T(8,128)S(1)}, f32[2,128,128]{2,1,0:T(8,128)}, u32[]{:S(2)}) copy-start(f32[2,128,128]{2,1,0:T(8,128)} %constant.22.clone.w_ref) | copy-start | bytes 393220
  0.0 13.1 %copy-start.4 = (f32[2,512]{1,0:T(2,128)S(1)}, f32[2,512]{1,0:T(2,128)}, u32[]{:S(2)}) copy-start(f32[2,512]{1,0:T(2,128)} %constant.23.clone.mid_ref) | copy-start | bytes 12292
  0.0 13.1 %copy-start.5 = (f32[8,128]{1,0:T(8,128)S(1)}, f32[8,128]{1,0:T(8,128)}, u32[]{:S(2)}) copy-start(f32[8,128]{1,0:T(8,128)} %constant.24.clone.lift_ref) | copy-start | bytes 12292
  0.0 13.1 %copy-start.2 = (bf16[256,384]{1,0:T(8,128)(2,1)S(1)}, bf16[256,384]{1,0:T(8,128)(2,1)}, u32[]{:S(2)}) copy-start(bf16[256,384]{1,0:T(8,128)(2,1)} %constant.25.clone.basis_ref) | copy-start | bytes 589828
  0.0 13.1 %copy-start.6 = (f32[512]{0:T(512)S(1)}, f32[512]{0:T(512)}, u32[]{:S(2)}) copy-start(f32[512]{0:T(512)} %constant.27.clone.wave_ref) | copy-start | bytes 6148
  5.5 16.3 %all-to-all-start = ((f32[16,48,128]{2,1,0:T(8,128)}), f32[16,48,128]{2,1,0:T(8,128)S(1)}, u32[]{:S(2)}, u32[]{:S(2)}) async-start(f32[16,48,128]{2,1,0:T(8,128)} %get-tuple-element.17), calls=%async_computation | async-start | bytes 786432 | tf_op jit(solution)/shard_map/all_to_all | solution.py:581
  13.1 20.0 %copy-start.1 = (bf16[768,256]{1,0:T(8,128)(2,1)S(1)}, bf16[768,256]{1,0:T(8,128)(2,1)}, u32[]{:S(2)}) copy-start(bf16[768,256]{1,0:T(8,128)(2,1)} %constant.21.clone.bwd_ref) | copy-start | bytes 1179652
  22.6 18.3 %all-to-all-start.1 = ((f32[16,8,128]{2,1,0:T(8,128)}), f32[16,8,128]{2,1,0:T(8,128)S(1)}, u32[]{:S(2)}, u32[]{:S(2)}) async-start(f32[16,8,128]{2,1,0:T(8,128)} %get-tuple-element.20), calls=%async_computation.1 | async-start | bytes 131072 | tf_op jit(solution)/shard_map/all_to_all | solution.py:581

commit v3 on v2

--- a/solution.py
+++ b/solution.py
@@ -22,9 +22,11 @@
 SUB = 8
 BLOCKS = TILE // SUB * PARTS
 BLOCK_PITCH = BLOCKS + 1
-LOADS = 8
+LOADS = 4
 CHUNK = 16
 STEPS = TILE // (2 * CHUNK)
+FORE = 32
+FORE_STEPS = TILE // (2 * FORE)
 MSG = 48
 LOW = 4
 
@@ -115,20 +117,19 @@
     return copies
 
 
-def side_start(t, side):
-    start = CHUNK * t if side == 0 else TILE - CHUNK * (t + 1)
-    return start if isinstance(start, int) else pl.multiple_of(start, CHUNK)
-
-
-def field_copies(x_ref, xv, sems, t, out=False):
+def side_start(t, side, chunk=CHUNK):
+    start = chunk * t if side == 0 else TILE - chunk * (t + 1)
+    return start if isinstance(start, int) else pl.multiple_of(start, chunk)
+
+
+def field_copies(x_ref, xv, sems, t):
     view = xv.reshape(PARTS, ROWS, PITCH, LANES)
     copies = []
     for side in range(2):
         for part in range(PARTS):
-            span = pl.ds(side_start(t, side), CHUNK)
+            span = pl.ds(side_start(t, side, FORE), FORE)
             ends = (x_ref.at[:, span, pl.ds(part * LANES, LANES)], view.at[part, :, span, :])
-            sem = sems.at[(2 * t + side) * PARTS + part]
-            copies.append(pltpu.make_async_copy(*(ends[::-1] if out else ends), sem))
+            copies.append(pltpu.make_async_copy(*ends, sems.at[(2 * t + side) * PARTS + part]))
     return copies
 
 
@@ -151,10 +152,10 @@
     return xv.reshape(ROWS * BLOCK_PITCH * SUB, LANES), pl.ds(start, ROWS, stride=BLOCK_PITCH * SUB)
 
 
-def row_copies(y_ref, yb, sems, t, out=False):
+def row_copies(y_ref, yb, sems, t, out=False, chunk=CHUNK):
     copies = []
     for side in range(2):
-        span = pl.ds(side_start(t, side) * ROWS, CHUNK * ROWS)
+        span = pl.ds(side_start(t, side, chunk) * ROWS, chunk * ROWS)
         ends = (y_ref.at[span, :], yb.at[span, :])
         copies.append(pltpu.make_async_copy(*(ends[::-1] if out else ends), sems.at[2 * t + side]))
     return copies
@@ -335,7 +336,7 @@
     x_ref, fwd_ref, w_ref, mid_ref, lift_ref, basis_ref, wave_ref, y_ref, ends_ref,
     xv, yb, in_sems, out_sems
 ):
-    for t in range(STEPS):
+    for t in range(FORE_STEPS):
         start_all(field_copies(x_ref, xv, in_sems, t))
     def loaded(a):
         return rows_at(xv, a) * PER_TURN
@@ -345,7 +346,7 @@
         here = loaded(start)
         above = turns(here - u)
         out, own = [], []
-        for i in range(CHUNK):
+        for i in range(FORE):
             own.append(here)
             after = loaded(jnp.minimum(start + i + 1, TILE - 1))
             below = turns(after - here)
@@ -366,25 +367,25 @@
         )
 
     def transform(t, low):
-        top, own_top = sources(t * CHUNK)
-        bottom, own_bottom = sources(TILE - CHUNK * (t + 1))
+        top, own_top = sources(t * FORE)
+        bottom, own_bottom = sources(TILE - FORE * (t + 1))
         stack = lambda u, v: jnp.concatenate([u[:, :TILE], u[:, TILE:], v[:, :TILE], v[:, TILE:]], 0)
         left = stack(own_top, own_bottom)
         both = jnp.dot(left, basis_ref[...], preferred_element_type=jnp.float32)
         kb, own = turns(both[:, :TILE]).astype(jnp.bfloat16), both[:, TILE:]
-        piece = lambda k, i: own[(k * CHUNK + i) * ROWS : (k * CHUNK + i + 1) * ROWS]
-        for i in range(CHUNK):
+        piece = lambda k, i: own[(k * FORE + i) * ROWS : (k * FORE + i + 1) * ROWS]
+        for i in range(FORE):
             pair = [
                 jnp.concatenate([piece(2 * side, j), piece(2 * side + 1, j)], 1)
-                for side, j in ((0, i), (1, CHUNK - 1 - i))
+                for side, j in ((0, i), (1, FORE - 1 - i))
             ]
-            low = gather_low(low, t * CHUNK + i, *pair)
+            low = gather_low(low, t * FORE + i, *pair)
         left = stack(top, bottom)
         left = jnp.concatenate([left, left, kb, kb], 1)
         y = jnp.dot(left, fwd_ref[...], preferred_element_type=jnp.float32)
-        size = CHUNK * ROWS
+        size = FORE * ROWS
         for side in range(2):
-            start = (t * CHUNK if side == 0 else TILE - CHUNK * (t + 1)) * ROWS
+            start = (t * FORE if side == 0 else TILE - FORE * (t + 1)) * ROWS
             start = pl.multiple_of(start, size)
             for c in range(COLS):
                 piece = y[(2 * side + c) * size : (2 * side + c + 1) * size]
@@ -393,8 +394,8 @@
 
     def eliminate(t, carry):
         top, bottom, low = carry
-        for i in range(CHUNK):
-            a = t * CHUNK + i
+        for i in range(FORE):
+            a = t * FORE + i
             scale = weight(w_ref, jnp.maximum(a - 1, 0))
             own_top, own_bottom = yb[at(a), :], yb[at(TILE - 1 - a), :]
             low = gather_low(low, a, narrow(own_top), narrow(own_bottom))
@@ -413,18 +414,18 @@
     def forward(t, carry):
         carry, low_z = carry
 
-        @pl.when(t + 1 < STEPS)
+        @pl.when(t + 1 < FORE_STEPS)
         def _():
             wait_all(field_copies(x_ref, xv, in_sems, t + 1))
 
         carry = eliminate(t - 1, carry)
         low_z = transform(t, low_z)
-        start_all(row_copies(y_ref, yb, out_sems, t - 1, out=True))
+        start_all(row_copies(y_ref, yb, out_sems, t - 1, out=True, chunk=FORE))
         return carry, low_z
 
-    carry, low_z = lax.fori_loop(1, STEPS, forward, ((zero, zero, none), low_z))
-    top, bottom, low_y = eliminate(STEPS - 1, carry)
-    start_all(row_copies(y_ref, yb, out_sems, STEPS - 1, out=True))
+    carry, low_z = lax.fori_loop(1, FORE_STEPS, forward, ((zero, zero, none), low_z))
+    top, bottom, low_y = eliminate(FORE_STEPS - 1, carry)
+    start_all(row_copies(y_ref, yb, out_sems, FORE_STEPS - 1, out=True, chunk=FORE))
     lift = []
     for p in range(LOW):
         rows = [
@@ -441,8 +442,8 @@
             ends_ref[(2 + p) * ROWS : (3 + p) * ROWS, c * TILE : c * TILE + LANES] = lift[p][
                 :, c * LANES : (c + 1) * LANES
             ]
-    for t in range(STEPS):
-        wait_all(row_copies(y_ref, yb, out_sems, t, out=True))
+    for t in range(FORE_STEPS):
+        wait_all(row_copies(y_ref, yb, out_sems, t, out=True, chunk=FORE))
 
 
 def backward_kernel(
@@ -619,8 +620,8 @@
         scratch_shapes=[
             pltpu.VMEM((PARTS, ROWS * PITCH, LANES), jnp.float32),
             pltpu.VMEM((ROWS * TILE, WIDTH), jnp.float32),
-            pltpu.SemaphoreType.DMA((2 * STEPS * PARTS,)),
-            pltpu.SemaphoreType.DMA((2 * STEPS,)),
+            pltpu.SemaphoreType.DMA((2 * FORE_STEPS * PARTS,)),
+            pltpu.SemaphoreType.DMA((2 * FORE_STEPS,)),
         ],
         compiler_params=pltpu.CompilerParams(vmem_limit_bytes=12 << 20),
         cost_estimate=pl.CostEstimate(flops=8 << 30, bytes_accessed=8 << 20, transcendentals=0),

time: 44.6 us -> 44.3 us (level)
  no operation moved by 1% of the time
where the time goes in v3:
time: 44.3 us; the launch traced here: 44.1 us
  Pallas kernels  25.5 us (58%)
  starting transfers between devices  18.3 us (41%)
    all_to_all x2, starting transfers between devices, to_all(): return lax.all_to_all(x, axis, 0, 0, tiled=True)  18.3 us
    pallas_call x1, Pallas kernels, per_device(): pl.pallas_call(forward_kernel, out_shape=(pltpu.HBM((ROWS * TILE, WIDTH),...  8.44 us
    pallas_call x1, Pallas kernels, per_device(): pl.pallas_call(backward_kernel, out_shape=(pltpu.HBM((ROWS, BLOCKS, SUB,...  7.66 us
    pallas_call x1, Pallas kernels, per_device(): pl.pallas_call(counts_kernel, out_shape=(f32(peers['col'], MSG, LANES), f...  5.19 us
    pallas_call x1, Pallas kernels, per_device(): pl.pallas_call(finish_kernel, out_shape=f32(ROWS, BLOCKS, SUB, LANES), in...  3.39 us
  transfers between devices with their start and end apart: 2, of which 1 were waited for; matrix products, arithmetic and copies ran while one was open for 0% of the time, Pallas kernels for 37%

profile of v3, /device:TPU:1, one launch (start us, length us, event | category | flops | bytes accessed | tf_op | source)
XLA Modules:
  0.0 44.1 jit_solution(1524405219538809879)
XLA Ops:
  0.0 0.0 copy-start
  0.0 0.0 copy-start.3
  0.0 0.0 copy-start.4
  0.0 0.0 copy-start.5
  0.0 0.0 copy-start.2
  0.0 0.0 copy-start.6
  0.0 5.2 %counts.1 = (f32[16,48,128]{2,1,0:T(8,128)}, f32[8,128]{1,0:T(8,128)S(1)}) custom-call(f32[8,256,512]{2,1,0:T(8,128)} %bitcast.11, f32[8,256]{1,0:T(8,128)} %constant.28.clone.edge_hbm, f32[1024]{0:T(1024)} %constant.29.clone.step_hbm, bf16[256,256]{1,0:T(8,128)(2,1)} %constant.26.clone.across_hbm), custom_call_target="tpu_custom_call" | custom-call | flops 1073741824 | bytes 4194304 | tf_op jit(solution)/shard_map/counts/pallas_call | solution.py:593
  5.2 7.6 %all-to-all-start = ((f32[16,48,128]{2,1,0:T(8,128)}), f32[16,48,128]{2,1,0:T(8,128)S(1)}, u32[]{:S(2)}, u32[]{:S(2)}) async-start(f32[16,48,128]{2,1,0:T(8,128)} %get-tuple-element.17), calls=%async_computation | async-start | bytes 786432 | tf_op jit(solution)/shard_map/all_to_all | solution.py:582
  12.8 0.0 copy-done
  12.9 0.0 copy-done.3
  12.9 0.0 copy-done.4
  12.9 0.0 copy-done.5
  12.9 0.0 copy-done.2
  12.9 0.0 copy-done.6
  12.9 0.0 copy-start.1
  12.9 8.4 %ahead.1 = (f32[2048,512]{1,0:T(8,128)}, f32[48,512]{1,0:T(8,128)S(1)}) custom-call(f32[8,256,512]{2,1,0:T(8,128)} %bitcast.12, bf16[1024,256]{1,0:T(8,128)(2,1)S(1)} %copy-done, f32[2,128,128]{2,1,0:T(8,128)S(1)} %copy-done.3, f32[2,512]{1,0:T(2,128)S(1)} %copy-done.4, f32[8,128]{1,0:T(8,128)S(1)} %copy-done.5, bf16[256,384]{1,0:T(8,128)(2,1)S(1)} %copy-done.2, ...), custom_call_target="tpu_custom_call" | custom-call | flops 8589934592 | bytes 8388608 | tf_op jit(solution)/shard_map/ahead/pallas_call | solution.py:615
  21.4 0.0 all-to-all-done.got_ref
  21.4 0.8 %across.1 = (f32[16,8,128]{2,1,0:T(8,128)}, f32[8,128]{1,0:T(8,128)S(1)}) custom-call(f32[16,48,128]{2,1,0:T(8,128)S(1)} %all-to-all-done.got_ref, f32[8,128]{1,0:T(8,128)S(1)} %get-tuple-element.18.loc_ref), custom_call_target="tpu_custom_call" | custom-call | tf_op jit(solution)/shard_map/across/pallas_call | solution.py:630
  22.2 10.7 %all-to-all-start.1 = ((f32[16,8,128]{2,1,0:T(8,128)}), f32[16,8,128]{2,1,0:T(8,128)S(1)}, u32[]{:S(2)}, u32[]{:S(2)}) async-start(f32[16,8,128]{2,1,0:T(8,128)} %get-tuple-element.20), calls=%async_computation.1 | async-start | bytes 131072 | tf_op jit(solution)/shard_map/all_to_all | solution.py:582
  32.9 0.0 copy-done.1
  32.9 7.7 %back.1 = (f32[8,128,8,128]{3,2,1,0:T(8,128)}, f32[8,256]{1,0:T(8,128)S(1)}) custom-call(f32[8,128,8,128]{3,2,1,0:T(8,128)} %bitcast.13, f32[2048,512]{1,0:T(8,128)} %get-tuple-element.13.y_ref, f32[48,512]{1,0:T(8,128)S(1)} %get-tuple-element.14.ends_ref, bf16[768,256]{1,0:T(8,128)(2,1)S(1)} %copy-done.1, f32[2,128,128]{2,1,0:T(8,128)S(1)} %copy-done.3, ...), custom_call_target="tpu_custom_call" | custom-call | flops 8589934592 | bytes 8388608 | tf_op jit(solution)/shard_map/back/pallas_call | solution.py:639
  40.6 0.1 all-to-all-done.1.down_ref
  40.7 3.4 %finish.1 = f32[8,128,8,128]{3,2,1,0:T(8,128)} custom-call(f32[8,128,8,128]{3,2,1,0:T(8,128)} %get-tuple-element.15.p_ref, f32[8,256]{1,0:T(8,128)S(1)} %get-tuple-element.16.sum_ref, f32[8,128]{1,0:T(8,128)S(1)} %get-tuple-element.19.part_ref, f32[16,8,128]{2,1,0:T(8,128)S(1)} %all-to-all-done.1.down_ref), custom_call_target="tpu_custom_call" | custom-call | tf_op jit(solution)/shard_map/finish/pallas_call | solution.py:658
Async XLA Ops:
  0.0 12.8 %copy-start = (bf16[1024,256]{1,0:T(8,128)(2,1)S(1)}, bf16[1024,256]{1,0:T(8,128)(2,1)}, u32[]{:S(2)}) copy-start(bf16[1024,256]{1,0:T(8,128)(2,1)} %constant.20.clone.fwd_ref) | copy-start | bytes 1572868
  0.0 12.9 %copy-start.3 = (f32[2,128,128]{2,1,0:T(8,128)S(1)}, f32[2,128,128]{2,1,0:T(8,128)}, u32[]{:S(2)}) copy-start(f32[2,128,128]{2,1,0:T(8,128)} %constant.22.clone.w_ref) | copy-start | bytes 393220
  0.0 12.9 %copy-start.4 = (f32[2,512]{1,0:T(2,128)S(1)}, f32[2,512]{1,0:T(2,128)}, u32[]{:S(2)}) copy-start(f32[2,512]{1,0:T(2,128)} %constant.23.clone.mid_ref) | copy-start | bytes 12292
  0.0 12.9 %copy-start.5 = (f32[8,128]{1,0:T(8,128)S(1)}, f32[8,128]{1,0:T(8,128)}, u32[]{:S(2)}) copy-start(f32[8,128]{1,0:T(8,128)} %constant.24.clone.lift_ref) | copy-start | bytes 12292
  0.0 12.9 %copy-start.2 = (bf16[256,384]{1,0:T(8,128)(2,1)S(1)}, bf16[256,384]{1,0:T(8,128)(2,1)}, u32[]{:S(2)}) copy-start(bf16[256,384]{1,0:T(8,128)(2,1)} %constant.25.clone.basis_ref) | copy-start | bytes 589828
  0.0 12.9 %copy-start.6 = (f32[512]{0:T(512)S(1)}, f32[512]{0:T(512)}, u32[]{:S(2)}) copy-start(f32[512]{0:T(512)} %constant.27.clone.wave_ref) | copy-start | bytes 6148
  5.2 16.1 %all-to-all-start = ((f32[16,48,128]{2,1,0:T(8,128)}), f32[16,48,128]{2,1,0:T(8,128)S(1)}, u32[]{:S(2)}, u32[]{:S(2)}) async-start(f32[16,48,128]{2,1,0:T(8,128)} %get-tuple-element.17), calls=%async_computation | async-start | bytes 786432 | tf_op jit(solution)/shard_map/all_to_all | solution.py:582
  12.9 20.0 %copy-start.1 = (bf16[768,256]{1,0:T(8,128)(2,1)S(1)}, bf16[768,256]{1,0:T(8,128)(2,1)}, u32[]{:S(2)}) copy-start(bf16[768,256]{1,0:T(8,128)(2,1)} %constant.21.clone.bwd_ref) | copy-start | bytes 1179652
  22.2 18.5 %all-to-all-start.1 = ((f32[16,8,128]{2,1,0:T(8,128)}), f32[16,8,128]{2,1,0:T(8,128)S(1)}, u32[]{:S(2)}, u32[]{:S(2)}) async-start(f32[16,8,128]{2,1,0:T(8,128)} %get-tuple-element.20), calls=%async_computation.1 | async-start | bytes 131072 | tf_op jit(solution)/shard_map/all_to_all | solution.py:582
